TPU v7x, 768 devices: a whole 4x8x12 slice. The times are simulated.
768 devices in a mesh: span: 12 (over z), shard: 64 (over x, y, core).
Axes of the slice: x: 4, y: 8, z: 12, core: 2. Of those that a mesh axis runs over, the one named last changes fastest.
Arguments:
- tokens: bfloat16 [196608, 1152], P(('span', 'shard')), may hold values from -6 to 6
- out_proj: bfloat16 [1152, 1152], replicated, may hold values from -0.1875 to 0.1875
- phi_mean: float32 [1152], replicated, may hold values from -6 to 6
- phi_rotate: bfloat16 [1152, 576], replicated, may hold values from -0.1875 to 0.1875
- destinations: int32 [196608, 1], P(('span', 'shard')), may hold values from 0 to 11; in each aligned block of 256 rows (0 to 255, 256 to 511, ...) at most 32 rows name the same one
- student_hidden: bfloat16 [294912, 1280], P(('span', 'shard')), may hold values from -6 to 6
- adaptor: bfloat16 [1280, 576], replicated, may hold values from -0.15625 to 0.15625
- master: float32 [1280, 576], P('shard'), may hold values from -0.15625 to 0.15625
- moment_one: float32 [1280, 576], P('shard'), may hold values from -4 to 4
- moment_two: float32 [1280, 576], P('shard'), may hold values from 0.01 to 1
Outputs:
- updated_master: float32 [1280, 576], P('shard')
- updated_first: float32 [1280, 576], P('shard')
- updated_second: float32 [1280, 576], P('shard')
Inputs may be any that keep to these rules, and one draw needn't show every extreme that they name: `destinations`: at most 32 of the 256 rows of one device name one span; some span gets exactly 32.
All inputs are finite; a program needn't handle non-finite values.
Results may differ from a plain program's by a relative error of at most 0.00064.
Values may be sent and summed in bfloat16 or wider, within the bound.
No kernel may reach another device: no remote copies, remote signals or barrier semaphores. Data moves between devices by JAX's collectives and lax.ppermute only.
A program may use at most 64 MiB of HBM per device.

v0:
```python
import jax
import jax.numpy as jnp
from jax import lax
from jax.sharding import PartitionSpec as P

ADAM_STEP = 1000


beta_first = 0.9
beta_second = 0.999
adam_epsilon = 1e-08
decay_rate = 0.05
learn_rate = 0.001


def in_blocks(x, dim, devices):
    shape = x.shape
    blocks = x.reshape(*shape[:dim], devices, shape[dim] // devices, *shape[dim + 1 :])
    return jnp.moveaxis(blocks, dim, 0)


def summed_on_arrival(x, axis, dim):
    blocks = in_blocks(x, dim, lax.axis_size(axis))
    arrived = lax.all_to_all(blocks, axis, split_axis=0, concat_axis=0, tiled=True)
    return arrived.sum(axis=0)


def copy_for_each(x, axis):
    copies = jnp.broadcast_to(x, (lax.axis_size(axis), *x.shape))
    return lax.all_to_all(copies, axis, split_axis=0, concat_axis=0, tiled=True)


def of_everyone(x, axis):
    return copy_for_each(x, axis).sum(axis=0)


def route_slots(destinations, span_count, capacity):
    target_span = destinations[:, 0]
    span_ids = jnp.arange(span_count, dtype=jnp.int32)
    one_hot = (target_span[:, None] == span_ids[None, :]).astype(jnp.int32)
    before = jnp.cumsum(one_hot, axis=0) - one_hot
    slot_rank = jnp.sum(before * one_hot, axis=1)
    counts_out = jnp.sum(one_hot, axis=0)
    return (target_span * capacity + slot_rank, counts_out)


def activate(values):
    return jax.nn.gelu(values.astype(jnp.float32), approximate=False).astype(jnp.bfloat16)


def adam_update(gradient, master, moment_one, moment_two):
    first_new = beta_first * moment_one + (1.0 - beta_first) * gradient
    second_new = beta_second * moment_two + (1.0 - beta_second) * gradient * gradient
    bias_first = 1.0 - beta_first**ADAM_STEP
    bias_second = 1.0 - beta_second**ADAM_STEP
    update_dir = (
        first_new / bias_first / (jnp.sqrt(second_new / bias_second) + adam_epsilon)
        + decay_rate * master
    )
    return (master - learn_rate * update_dir, first_new, second_new)


def reduce_and_step(activated, scaled_error, master, moment_one, moment_two):
    contract = (((0,), (0,)), ((), ()))
    partial_sum = summed_on_arrival(
        lax.dot_general(activated, scaled_error, contract, preferred_element_type=jnp.float32),
        "shard",
        0,
    )
    gradient = of_everyone(partial_sum, "span")
    return adam_update(gradient, master, moment_one, moment_two)


def body(
    tokens,
    out_proj,
    phi_mean,
    phi_rotate,
    destinations,
    student_hidden,
    adaptor,
    master,
    moment_one,
    moment_two,
):
    span_count = lax.axis_size("span")
    capacity = student_hidden.shape[0] // span_count
    feature_count = adaptor.shape[1]
    projected = (jnp.dot(tokens, out_proj, preferred_element_type=jnp.float32) - phi_mean).astype(
        jnp.bfloat16
    )
    teacher_target = jnp.dot(projected, phi_rotate, preferred_element_type=jnp.float32).astype(
        jnp.bfloat16
    )
    slot_ids, counts_out = route_slots(destinations, span_count, capacity)
    outgoing = (
        jnp.zeros((span_count * capacity, feature_count), jnp.bfloat16)
        .at[slot_ids]
        .set(teacher_target)
    )
    arrived, arrived_counts = (
        lax.all_to_all(
            outgoing.reshape(span_count, capacity, feature_count),
            "span",
            split_axis=0,
            concat_axis=0,
            tiled=True,
        ),
        lax.all_to_all(
            counts_out.reshape(span_count, 1), "span", split_axis=0, concat_axis=0, tiled=True
        ),
    )
    live_slots = (jnp.arange(capacity, dtype=jnp.int32)[None, :] < arrived_counts).reshape(-1, 1)
    activated = activate(student_hidden)
    predicted = jnp.dot(activated, adaptor, preferred_element_type=jnp.float32)
    arrived_flat = arrived.reshape(span_count * capacity, feature_count).astype(jnp.float32)
    error_value = jnp.where(live_slots, predicted - arrived_flat, 0.0)
    scaled_error = (error_value / feature_count).astype(jnp.bfloat16)
    return reduce_and_step(activated, scaled_error, master, moment_one, moment_two)


def solution(mesh):
    in_specs = (
        P(("span", "shard"), None),
        P(),
        P(),
        P(),
        P(("span", "shard"), None),
        P(("span", "shard"), None),
        P(),
        P("shard", None),
        P("shard", None),
        P("shard", None),
    )
    out_specs = (P("shard", None), P("shard", None), P("shard", None))
    return jax.shard_map(body, mesh=mesh, in_specs=in_specs, out_specs=out_specs, check_vma=False)
```

profile of v0, /device:TPU:65, one launch (start us, length us, event | category | flops | bytes accessed | tf_op | source)
XLA Modules:
  0.0 216.6 jit_solution(9714608649414678959)
XLA Ops:
  0.6 0.0 copy-start
  0.6 0.8 fusion.101
  1.5 0.6 reduce-window.6
  2.1 0.2 slice_reduce_fusion
  2.3 0.1 broadcast_add_fusion
  2.4 0.8 convert_reduce_fusion
  3.2 0.7 copy.26
  3.9 14.2 %all-to-all-start = ((s32[12,1,1]{2,1,0:T(1,128)}), s32[12,1,1]{2,1,0:T(1,128)S(1)}, u32[]{:S(2)}, u32[]{:S(2)}) async-start(s32[12,1,1]{2,1,0:T(1,128)} %copy.26), calls=%async_computation | async-start | bytes 12288 | tf_op jit(solution)/shard_map/all_to_all | solution.py:109
  18.1 0.7 compare_select_fusion
  18.8 0.0 copy-done
  18.8 3.0 %convolution_convert_fusion = bf16[256,576]{0,1:T(8,128)(2,1)S(1)} fusion(bf16[1152,576]{0,1:T(8,128)(2,1)} %param.13, bf16[256,1152]{1,0:T(8,128)(2,1)} %param.10, bf16[1152,1152]{1,0:T(8,128)(2,1)S(1)} %copy-done, f32[1152]{0:T(1024)} %param.12), kind=kOutput, calls=%fused_computation.41 | convolution fusion | flops 1019953152 | bytes 4870656 | tf_op jit(solution)/shard_map/dot_general | solution.py:92
  21.8 0.2 copy.28
  22.0 2.4 %scatter_custom_fusion = bf16[384,576]{1,0:T(8,128)(2,1)} fusion(s32[256]{0:T(256)S(1)} %bitcast.25, bf16[256,576]{1,0:T(8,128)(2,1)S(1)} %copy.28, bf16[]{:T(256)} %constant.33.clone.1), kind=kCustom, calls=%fused_computation.75 | custom fusion | bytes 442370 | tf_op jit(solution)/shard_map/scatter | solution.py:99
  24.4 1.4 all-to-all-done
  25.8 7.6 %all-to-all-start.1 = ((bf16[12,32,576]{2,1,0:T(8,128)(2,1)}), bf16[12,32,576]{2,1,0:T(8,128)(2,1)S(1)}, u32[]{:S(2)}, u32[]{:S(2)}) async-start(bf16[12,32,576]{2,1,0:T(8,128)(2,1)} %bitcast.6), calls=%async_computation.1 | async-start | bytes 983040 | tf_op jit(solution)/shard_map/all_to_all | solution.py:102
  33.5 0.3 reduce
  33.8 0.1 iota_compare_fusion.2
  33.8 0.1 lt.33
  33.9 23.2 %all-to-all-done.1 = bf16[12,32,576]{2,1,0:T(8,128)(2,1)S(1)} async-done(((bf16[12,32,576]{2,1,0:T(8,128)(2,1)}), bf16[12,32,576]{2,1,0:T(8,128)(2,1)S(1)}, u32[]{:S(2)}, u32[]{:S(2)}) %all-to-all-start.1) | async-done | bytes 442400 | tf_op jit(solution)/shard_map/all_to_all | solution.py:102
  57.1 1.1 bitcast_convert_fusion
  58.2 1.5 copy.29
  59.7 13.1 %fusion.35 = f32[1280,576]{1,0:T(8,128)} fusion(f32[384,576]{0,1:T(8,128)S(1)} %copy.29, bf16[1280,576]{0,1:T(8,128)(2,1)} %param.16, bf16[384,1280]{1,0:T(8,128)(2,1)} %param.15, pred[384]{0:T(512)(128)(4,1)S(1)} %lt.33), kind=kOutput, calls=%fused_computation.42 | convolution fusion | flops 1198227456 | bytes 6291840 | tf_op jit(solution)/shard_map/dot_general | solution.py:66
  72.8 4.6 %reshape.55 = f32[64,20,576]{2,1,0:T(8,128)} reshape(f32[1280,576]{1,0:T(8,128)} %fusion.35) | data formatting | bytes 5898240 | tf_op jit(solution)/shard_map/reshape | solution.py:18
  77.4 101.1 %all_to_all.24 = f32[64,20,576]{2,1,0:T(8,128)} all-to-all(f32[64,20,576]{2,1,0:T(8,128)} %reshape.55), channel_id=1, replica_groups=mesh['span'=12,'shard'=64] {'shard'}, dimensions={0} | all-to-all | bytes 5898240 | tf_op jit(solution)/shard_map/all_to_all | solution.py:24
  178.5 2.4 %reduce_sum.41 = f32[20,576]{1,0:T(8,128)S(1)} reduce(f32[64,20,576]{2,1,0:T(8,128)} %all_to_all.24, f32[]{:T(128)} %constant.12.clone.1), dimensions={0}, to_apply=%region_5.6 | reduce | flops 725760 | bytes 2995204 | tf_op jit(solution)/shard_map/reduce_sum | solution.py:25
  180.9 0.0 copy-start.1
  180.9 34.0 %all_to_all.25 = f32[12,20,576]{2,1,0:T(8,128)S(1)} all-to-all(f32[12,20,576]{2,1,0:T(8,128)S(1)} %broadcast_in_dim.25), channel_id=1, replica_groups=mesh['span'=12,'shard'=64] {'span'}, dimensions={0} | all-to-all | bytes 1105920 | tf_op jit(solution)/shard_map/all_to_all | solution.py:30
  215.0 0.0 copy-done.1
  215.0 1.5 multiply_subtract_fusion
  (7 shorter events, 0.2 us)
Async XLA Ops:
  0.6 18.2 %copy-start = (bf16[1152,1152]{1,0:T(8,128)(2,1)S(1)}, bf16[1152,1152]{1,0:T(8,128)(2,1)}, u32[]{:S(2)}) copy-start(bf16[1152,1152]{1,0:T(8,128)(2,1)} %param.11) | copy-start | bytes 7962628
  3.9 21.9 %all-to-all-start = ((s32[12,1,1]{2,1,0:T(1,128)}), s32[12,1,1]{2,1,0:T(1,128)S(1)}, u32[]{:S(2)}, u32[]{:S(2)}) async-start(s32[12,1,1]{2,1,0:T(1,128)} %copy.26), calls=%async_computation | async-start | bytes 12288 | tf_op jit(solution)/shard_map/all_to_all | solution.py:109
  25.8 31.3 %all-to-all-start.1 = ((bf16[12,32,576]{2,1,0:T(8,128)(2,1)}), bf16[12,32,576]{2,1,0:T(8,128)(2,1)S(1)}, u32[]{:S(2)}, u32[]{:S(2)}) async-start(bf16[12,32,576]{2,1,0:T(8,128)(2,1)} %bitcast.6), calls=%async_computation.1 | async-start | bytes 983040 | tf_op jit(solution)/shard_map/all_to_all | solution.py:102
  180.9 34.1 %copy-start.1 = (f32[20,576]{1,0:T(8,128)S(1)}, f32[20,576]{1,0:T(8,128)}, u32[]{:S(2)}) copy-start(f32[20,576]{1,0:T(8,128)} %param.17) | copy-start | bytes 138244
where the time goes:
time: 217 us
  blocking collectives  135 us (62%)
  waiting for transfers between devices  24.6 us (11%)
  starting transfers between devices  21.8 us (10%)
  matrix products  16.1 us (7%)
  local copies, waits for them, and re-layouts  9.77 us (5%)
  other arithmetic  8.4 us (4%)
    all_to_all x1, blocking collectives, summed_on_arrival(): lax.all_to_all(blocks, axis, split_axis=0, concat_axis=0, tiled=True)  101 us
    all_to_all x1, blocking collectives, copy_for_each(): return lax.all_to_all(copies, axis, split_axis=0, concat_axis=0, tiled=True)  34 us
    all_to_all x1, waiting for transfers between devices, body(): lax.all_to_all(outgoing.reshape(span_count, capacity, feature_count), 'sp...  23.2 us
    all_to_all x1, starting transfers between devices, body(): lax.all_to_all(counts_out.reshape(span_count, 1), 'span', split_axis=0, c...  14.2 us
    dot_general x1, matrix products, reduce_and_step(): lax.dot_general(activated, scaled_error, contract, preferred_element_type...  13.1 us
    all_to_all x1, starting transfers between devices, body(): lax.all_to_all(outgoing.reshape(span_count, capacity, feature_count), 'sp...  7.62 us
    reshape x1, local copies, waits for them, and re-layouts, in_blocks(): x.reshape(*shape[:dim], devices, shape[dim] // devices, *shape[dim + 1:])  4.61 us
  transfers between devices with their start and end apart: 2, of which 2 were waited for; matrix products, arithmetic and copies ran while one was open for 3% of the time, Pallas kernels for 0%

commit v1 on v0

v1 whole, which is shorter than its diff:
```python
import functools

import jax
import jax.numpy as jnp
from jax import lax
from jax.experimental import pallas as pl
from jax.experimental.pallas import tpu as pltpu
from jax.sharding import Mesh, PartitionSpec as P

ADAM_STEP = 1000
beta_first = 0.9
beta_second = 0.999
adam_epsilon = 1e-08
decay_rate = 0.05
learn_rate = 0.001

NZ, NX, NY, NC = 12, 4, 8, 2
CAP = 32
ROWS = 256
SLOTS = NZ * CAP
H = 1280
DW = 576
WIDE = 640
OWN = H // (NX * NY * NC)
HALF = H // NC
XB = HALF // NX
TILE_ROWS = NZ * 8
f32 = jnp.float32
bf16 = jnp.bfloat16
YZ_TYPE = bf16


def call(kernel, outs, args, scratch=(), vmem=24, specs=None, flops=0, moved=0):
    return pl.pallas_call(
        kernel,
        out_shape=outs,
        in_specs=specs or [pl.BlockSpec()] * len(args),
        scratch_shapes=list(scratch),
        compiler_params=pltpu.CompilerParams(vmem_limit_bytes=vmem * 2**20),
        cost_estimate=pl.CostEstimate(flops=flops, bytes_accessed=moved, transcendentals=0),
    )(*args)


def route_kernel(dest_ref, rows_ref, out_ref):
    dest = dest_ref[...]
    spans = lax.broadcasted_iota(jnp.int32, (16, ROWS), 0)
    named = spans == dest
    one_hot = jnp.where(named, 1.0, 0.0)
    earlier = (
        lax.broadcasted_iota(jnp.int32, (ROWS, ROWS), 0)
        < lax.broadcasted_iota(jnp.int32, (ROWS, ROWS), 1)
    )
    before = jnp.dot(
        one_hot.astype(bf16),
        jnp.where(earlier, 1.0, 0.0).astype(bf16),
        preferred_element_type=f32,
    )
    rank = jnp.sum(before * one_hot, axis=0, keepdims=True)
    slot = dest * CAP + rank.astype(jnp.int32)
    place = lax.broadcasted_iota(jnp.int32, (SLOTS, ROWS), 0) == slot
    out_ref[...] = jnp.dot(
        jnp.where(place, 1.0, 0.0).astype(bf16), rows_ref[...], preferred_element_type=f32
    ).astype(bf16)


def student_kernel(core_ref, act_ref, adaptor_t_ref, pred_ref, send_ref, keep_ref):
    nt = (((1,), (1,)), ((), ()))
    act = act_ref[...]
    pred_ref[...] = lax.dot_general(act, adaptor_t_ref[...], nt, preferred_element_type=f32)
    core = core_ref[0]
    place = lax.broadcasted_iota(jnp.int32, (HALF, 1), 0)
    unit = place + OWN * (place // OWN)
    column = lax.broadcasted_iota(jnp.int32, (HALF, H), 1)
    for ref, owner in ((send_ref, 1 - core), (keep_ref, core)):
        pick = jnp.where(column == unit + OWN * owner, 1.0, 0.0).astype(bf16)
        ref[...] = lax.dot_general(pick, act, nt, preferred_element_type=f32).astype(bf16)


def error_kernel(arrived_ref, pred_ref, send_ref, error_ref, out_ref):
    live = arrived_ref[:, DW : DW + 1].astype(f32) > 0.5
    error = jnp.where(live, pred_ref[...] - arrived_ref[:, :DW].astype(f32), 0.0)
    error = (error / DW).astype(bf16)
    error_ref[...] = error
    out_ref[:, :DW] = jnp.dot(send_ref[...], error, preferred_element_type=f32).astype(bf16)
    out_ref[:, DW:] = jnp.zeros((HALF, WIDE - DW), bf16)


def keep_kernel(keep_ref, error_ref, out_ref):
    out_ref[...] = jnp.dot(keep_ref[...], error_ref[...], preferred_element_type=f32)


def add_kernel(own_ref, got_ref, out_ref):
    out_ref[...] = (own_ref[...] + got_ref[:, :DW].astype(f32)).astype(bf16)


def tile_kernel(got_ref, out_ref, sum_ref, flat_ref):
    total = got_ref[0].astype(f32)
    for x in range(1, NX):
        total = total + got_ref[x].astype(f32)
    sum_ref[:, :DW] = total
    sum_ref[:, DW:] = jnp.zeros((XB, WIDE - DW), f32)
    left = lax.broadcasted_iota(jnp.int32, (OWN // 2, 128), 1) < 64
    for y in range(NY):
        at, to = y * OWN, y * TILE_ROWS
        for l in range(4):
            flat_ref[to + l * OWN : to + (l + 1) * OWN, :] = sum_ref[
                at : at + OWN, l * 128 : (l + 1) * 128
            ]
        upper = sum_ref[at : at + OWN // 2, 512:640]
        lower = pltpu.roll(sum_ref[at + OWN // 2 : at + OWN, 512:640], 64, axis=1)
        flat_ref[to + 80 : to + 90, :] = jnp.where(left, upper, lower)
        flat_ref[to + 90 : to + 96, :] = jnp.zeros((6, 128), f32)
        for z in range(NZ):
            out_ref[z * NY + y] = flat_ref[to + z * 8 : to + z * 8 + 8, :].astype(out_ref.dtype)


def adam_kernel(tiles_ref, master_ref, one_ref, two_ref, m_out, f_out, s_out, grad_ref):
    for l in range(4):
        grad_ref[:, l * 128 : (l + 1) * 128] = tiles_ref[l * OWN : (l + 1) * OWN, :]
    last = tiles_ref[80:90, :]
    grad_ref[0:10, 512:640] = last
    grad_ref[10:20, 512:640] = pltpu.roll(last, 64, axis=1)
    gradient = grad_ref[:, :DW]
    master = master_ref[...]
    first_new = beta_first * one_ref[...] + (1.0 - beta_first) * gradient
    second_new = beta_second * two_ref[...] + (1.0 - beta_second) * gradient * gradient
    bias_first = 1.0 - beta_first**ADAM_STEP
    bias_second = 1.0 - beta_second**ADAM_STEP
    update_dir = (
        first_new / bias_first / (jnp.sqrt(second_new / bias_second) + adam_epsilon)
        + decay_rate * master
    )
    m_out[...] = master - learn_rate * update_dir
    f_out[...] = first_new
    s_out[...] = second_new


def exchange(x, axis):
    return lax.all_to_all(x, axis, split_axis=0, concat_axis=0, tiled=True)


def body(
    tokens,
    out_proj,
    phi_mean,
    phi_rotate,
    destinations,
    student_hidden,
    adaptor,
    master,
    moment_one,
    moment_two,
):
    shape = jax.ShapeDtypeStruct
    projected = (jnp.dot(tokens, out_proj, preferred_element_type=f32) - phi_mean).astype(bf16)
    target = jnp.dot(projected, phi_rotate, preferred_element_type=f32).astype(bf16)
    marked = jnp.pad(target, ((0, 0), (0, WIDE - DW)), constant_values=1.0)
    outgoing = call(
        route_kernel,
        shape((SLOTS, WIDE), bf16),
        (destinations.reshape(1, ROWS), marked),
        flops=2 * SLOTS * ROWS * WIDE,
        moved=2 * WIDE * (SLOTS + ROWS),
    )
    arrived = exchange(outgoing.reshape(NZ, CAP, WIDE), "z").reshape(SLOTS, WIDE)

    activated = jax.nn.gelu(student_hidden.astype(f32), approximate=False).astype(bf16)
    core = lax.axis_index("c").astype(jnp.int32).reshape(1)
    whole = pl.BlockSpec()
    predicted, act_send, act_keep = call(
        student_kernel,
        (shape((SLOTS, DW), f32), shape((HALF, SLOTS), bf16), shape((HALF, SLOTS), bf16)),
        (core, activated, adaptor.T),
        specs=[pl.BlockSpec(memory_space=pltpu.SMEM), whole, whole],
        flops=2 * SLOTS * H * (DW + H),
        moved=2 * SLOTS * H * 2 + 2 * H * DW + 4 * SLOTS * DW,
    )
    error, for_partner = call(
        error_kernel,
        (shape((SLOTS, DW), bf16), shape((HALF, WIDE), bf16)),
        (arrived, predicted, act_send),
        flops=2 * SLOTS * HALF * DW,
        moved=2 * SLOTS * (WIDE + 3 * DW + HALF) + 2 * HALF * DW,
    )
    from_partner = lax.ppermute(for_partner, "c", [(0, 1), (1, 0)])
    own = call(
        keep_kernel,
        shape((HALF, DW), f32),
        (act_keep, error),
        flops=2 * SLOTS * HALF * DW,
        moved=2 * SLOTS * (DW + HALF) + 4 * HALF * DW,
    )
    chip_sum = call(
        add_kernel, shape((HALF, DW), bf16), (own, from_partner), moved=8 * HALF * DW
    )
    by_x = exchange(chip_sum.reshape(NX, XB, DW), "x")
    tiles = call(
        tile_kernel,
        shape((NZ * NY, 8, 128), YZ_TYPE),
        (by_x,),
        scratch=(pltpu.VMEM((XB, WIDE), f32), pltpu.VMEM((NY * TILE_ROWS, 128), f32)),
        moved=4 * XB * DW * 4,
    )
    by_yz = exchange(tiles, ("z", "y"))
    part = by_yz.astype(f32).sum(axis=0)
    gathered = exchange(jnp.broadcast_to(part, (NZ, 8, 128)), "z").reshape(TILE_ROWS, 128)
    out = shape((OWN, DW), f32)
    return call(
        adam_kernel,
        (out, out, out),
        (gathered, master, moment_one, moment_two),
        scratch=(pltpu.VMEM((OWN, WIDE), f32),),
        moved=4 * OWN * DW * 7,
    )


def solution(mesh):
    grid = Mesh(mesh.devices.reshape(NZ, NX, NY, NC), ("z", "x", "y", "c"))
    shard = ("x", "y", "c")
    rows = P(("z", "x", "y", "c"), None)
    state = P(shard, None)
    in_specs = (rows, P(), P(), P(), rows, rows, P(), state, state, state)
    return jax.shard_map(
        body, mesh=grid, in_specs=in_specs, out_specs=(state, state, state), check_vma=False
    )
```

time: 217 us -> 111 us (0.51)
  the two profiles are of different devices: /device:TPU:65 before, /device:TPU:8 now
where the time goes in v1:
time: 111 us; the launch traced here: 110 us
  blocking collectives  57.2 us (52%)
  starting transfers between devices  17.1 us (15%)
  waiting for transfers between devices  13.6 us (12%)
  local copies, waits for them, and re-layouts  6.77 us (6%)
  Pallas kernels  6.37 us (6%)
  other arithmetic  5.48 us (5%)
  matrix products  2.99 us (3%)
    all_to_all x3, blocking collectives, exchange(): return lax.all_to_all(x, axis, split_axis=0, concat_axis=0, tiled=True)  57.2 us
    all_to_all x1, starting transfers between devices, exchange(): return lax.all_to_all(x, axis, split_axis=0, concat_axis=0, tiled=True)  15.2 us
    all_to_all x1, waiting for transfers between devices, exchange(): return lax.all_to_all(x, axis, split_axis=0, concat_axis=0, tiled=True)  11.9 us
    unnamed x24, local copies, waits for them, and re-layouts  6.53 us
    pallas_call x7, Pallas kernels, call(): pl.pallas_call(kernel, out_shape=outs, in_specs=specs or [pl.BlockSpec()]...  6.37 us
    convert_element_type x1, other arithmetic, body(): jax.nn.gelu(student_hidden.astype(f32), approximate=False).astype(bf16)  5.38 us
    dot_general x1, matrix products, body(): jnp.dot(projected, phi_rotate, preferred_element_type=f32).astype(bf16)  2.99 us
  transfers between devices with their start and end apart: 2, of which 2 were waited for; matrix products, arithmetic and copies ran while one was open for 5% of the time, Pallas kernels for 3%

profile of v1, /device:TPU:8, one launch (start us, length us, event | category | flops | bytes accessed | tf_op | source)
XLA Modules:
  0.0 110.3 jit_solution(7827294498702418593)
XLA Ops:
  0.6 0.0 copy-start
  0.6 0.0 copy-start.10
  0.7 1.7 %copy-done = bf16[1152,1152]{1,0:T(8,128)(2,1)S(1)} copy-done((bf16[1152,1152]{1,0:T(8,128)(2,1)S(1)}, bf16[1152,1152]{1,0:T(8,128)(2,1)}, u32[]{:S(2)}) %copy-start) | copy-done | bytes 2654232
  2.4 3.0 %convolution_convert_fusion = bf16[256,576]{0,1:T(8,128)(2,1)S(1)} fusion(bf16[1152,576]{0,1:T(8,128)(2,1)} %param.13, bf16[256,1152]{1,0:T(8,128)(2,1)} %param.10, bf16[1152,1152]{1,0:T(8,128)(2,1)S(1)} %copy-done, f32[1152]{0:T(1024)} %param.12), kind=kOutput, calls=%fused_computation.36 | convolution fusion | flops 1019953152 | bytes 4870656 | tf_op jit(solution)/shard_map/dot_general | solution.py:156
  5.4 0.2 copy.14
  5.6 0.0 copy-done.10
  5.6 1.3 %shard_map.122 = bf16[384,640]{1,0:T(8,128)(2,1)} custom-call(s32[1,256]{1,0:T(1,128)S(1)} %bitcast.13, bf16[256,640]{1,0:T(8,128)(2,1)S(1)} %pad.4.rows_ref), custom_call_target="tpu_custom_call" | custom-call | flops 125829120 | bytes 819200 | tf_op jit(solution)/shard_map/pallas_call | solution.py:34
  6.9 15.2 %all-to-all-start = ((bf16[12,32,640]{2,1,0:T(8,128)(2,1)}), bf16[12,32,640]{2,1,0:T(8,128)(2,1)S(1)}, u32[]{:S(2)}, u32[]{:S(2)}) async-start(bf16[12,32,640]{2,1,0:T(8,128)(2,1)} %bitcast.3), calls=%async_computation | async-start | bytes 983040 | tf_op jit(solution)/shard_map/all_to_all | solution.py:139
  22.1 0.0 copy-start.11
  22.1 5.4 %fusion.2.act_ref = bf16[384,1280]{1,0:T(8,128)(2,1)S(1)} fusion(bf16[384,1280]{1,0:T(8,128)(2,1)} %param.15), kind=kLoop, calls=%fused_computation.6 | loop fusion | flops 32440320 | bytes 1966080 | tf_op jit(solution)/shard_map/convert_element_type | solution.py:167
  27.5 0.0 copy-done.11
  27.5 2.7 %shard_map.121 = (f32[384,576]{1,0:T(8,128)S(1)}, bf16[640,384]{1,0:T(8,128)(2,1)S(1)}, bf16[640,384]{1,0:T(8,128)(2,1)S(1)}) custom-call(s32[1]{0:T(128)} %bitcast.core_ref, bf16[384,1280]{1,0:T(8,128)(2,1)S(1)} %fusion.2.act_ref, bf16[576,1280]{1,0:T(8,128)(2,1)S(1)} %bitcast.14), custom_call_target="tpu_custom_call" | custom-call | flops 1824522240 | bytes 4325376 | tf_op jit(solution)/shard_map/pallas_call | solution.py:34
  30.1 0.0 copy-start.1
  30.2 0.9 copy-done.1
  31.1 0.0 copy-start.3
  31.1 0.8 copy-done.3
  31.9 0.0 copy-start.5
  31.9 0.8 copy-done.5
  32.7 11.9 %all-to-all-done = bf16[12,32,640]{2,1,0:T(8,128)(2,1)S(1)} async-done(((bf16[12,32,640]{2,1,0:T(8,128)(2,1)}), bf16[12,32,640]{2,1,0:T(8,128)(2,1)S(1)}, u32[]{:S(2)}, u32[]{:S(2)}) %all-to-all-start) | async-done | bytes 491552 | tf_op jit(solution)/shard_map/all_to_all | solution.py:139
  44.6 0.0 copy-start.2
  44.6 1.2 %copy-done.2 = f32[384,576]{1,0:T(8,128)S(1)} copy-done((f32[384,576]{1,0:T(8,128)S(1)}, f32[384,576]{1,0:T(8,128)}, u32[]{:S(2)}) %copy-start.2) | copy-done | bytes 884760
  45.8 0.0 copy-start.6
  45.8 1.0 copy-done.6
  46.9 0.0 copy-start.4
  46.9 0.8 shard_map.123
  47.6 1.9 %collective-permute-start = (bf16[640,640]{1,0:T(8,128)(2,1)S(1)}, bf16[640,640]{1,0:T(8,128)(2,1)S(1)}, u32[]{:S(2)}, u32[]{:S(2)}) collective-permute-start(bf16[640,640]{1,0:T(8,128)(2,1)S(1)} %get-tuple-element.12), channel_id=1, source_target_pairs={{0,1},{1,0},{2,3},{3,2},{4,5},{5,4},{6,7},{7,6},{8,9},{9,8},{10,11... | collective-permute-start | bytes 2457608 | tf_op jit(solution)/shard_map/ppermute | solution.py:185
  49.6 0.0 copy-done.4
  49.6 0.6 shard_map.124.own_ref
  50.2 1.7 %collective-permute-done.got_ref = bf16[640,640]{1,0:T(8,128)(2,1)S(1)} collective-permute-done((bf16[640,640]{1,0:T(8,128)(2,1)S(1)}, bf16[640,640]{1,0:T(8,128)(2,1)S(1)}, u32[]{:S(2)}, u32[]{:S(2)}) %collective-permute-start) | collective-permute-done | bytes 819232 | tf_op jit(solution)/shard_map/ppermute | solution.py:185
  51.9 0.1 shard_map.125
  52.0 0.0 copy-start.7
  52.0 0.0 copy-start.8
  52.0 0.0 copy-start.9
  52.0 17.2 %all_to_all.20.got_ref = bf16[4,160,576]{2,1,0:T(8,128)(2,1)S(1)} all-to-all(bf16[4,160,576]{2,1,0:T(8,128)(2,1)S(1)} %bitcast.10), channel_id=1, replica_groups=mesh['z'=12,'x'=4,'y'=8,'c'=2] {'x'}, dimensions={0} | all-to-all | bytes 1474560 | tf_op jit(solution)/shard_map/all_to_all | solution.py:139
  69.2 0.2 shard_map.126
  69.4 26.6 %all_to_all.21 = bf16[96,8,128]{2,1,0:T(8,128)(2,1)S(1)} all-to-all(bf16[96,8,128]{2,1,0:T(8,128)(2,1)S(1)} %shard_map.126), channel_id=1, replica_groups=mesh['z'=12,'x'=4,'y'=8,'c'=2] {'z','y'}, dimensions={0} | all-to-all | bytes 393216 | tf_op jit(solution)/shard_map/all_to_all | solution.py:139
  96.0 0.1 convert_reduce_fusion
  96.1 13.5 %all_to_all.22 = f32[12,8,128]{2,1,0:T(8,128)S(1)} all-to-all(f32[12,8,128]{2,1,0:T(8,128)S(1)} %broadcast_in_dim.4), channel_id=1, replica_groups=mesh['z'=12,'x'=4,'y'=8,'c'=2] {'z'}, dimensions={0} | all-to-all | bytes 98304 | tf_op jit(solution)/shard_map/all_to_all | solution.py:139
  109.5 0.0 copy-done.7
  109.6 0.0 copy-done.8
  109.6 0.0 copy-done.9
  109.6 0.7 shard_map.127
  (2 shorter events, 0.0 us)
Async XLA Ops:
  0.6 1.8 %copy-start = (bf16[1152,1152]{1,0:T(8,128)(2,1)S(1)}, bf16[1152,1152]{1,0:T(8,128)(2,1)}, u32[]{:S(2)}) copy-start(bf16[1152,1152]{1,0:T(8,128)(2,1)} %param.11) | copy-start | bytes 7962628
  0.6 5.0 %copy-start.10 = (s32[256,1]{0,1:T(1,128)S(1)}, s32[256,1]{0,1:T(1,128)}, u32[]{:S(2)}) copy-start(s32[256,1]{0,1:T(1,128)} %param.14) | copy-start | bytes 3076
  6.9 37.7 %all-to-all-start = ((bf16[12,32,640]{2,1,0:T(8,128)(2,1)}), bf16[12,32,640]{2,1,0:T(8,128)(2,1)S(1)}, u32[]{:S(2)}, u32[]{:S(2)}) async-start(bf16[12,32,640]{2,1,0:T(8,128)(2,1)} %bitcast.3), calls=%async_computation | async-start | bytes 983040 | tf_op jit(solution)/shard_map/all_to_all | solution.py:139
  22.1 5.4 %copy-start.11 = (bf16[1280,576]{0,1:T(8,128)(2,1)S(1)}, bf16[1280,576]{0,1:T(8,128)(2,1)}, u32[]{:S(2)}) copy-start(bf16[1280,576]{0,1:T(8,128)(2,1)} %param.16) | copy-start | bytes 4423684
  30.1 1.0 copy-start.1
  31.1 0.8 copy-start.3
  31.9 0.8 copy-start.5
  44.6 1.2 %copy-start.2 = (f32[384,576]{1,0:T(8,128)S(1)}, f32[384,576]{1,0:T(8,128)}, u32[]{:S(2)}) copy-start(f32[384,576]{1,0:T(8,128)} %copy-done.1) | copy-start | bytes 2654212
  45.8 1.0 copy-start.6
  46.9 2.7 %copy-start.4 = (bf16[640,384]{1,0:T(8,128)(2,1)S(1)}, bf16[640,384]{1,0:T(8,128)(2,1)}, u32[]{:S(2)}) copy-start(bf16[640,384]{1,0:T(8,128)(2,1)} %copy-done.3) | copy-start | bytes 1474564
  47.6 4.2 %collective-permute-start = (bf16[640,640]{1,0:T(8,128)(2,1)S(1)}, bf16[640,640]{1,0:T(8,128)(2,1)S(1)}, u32[]{:S(2)}, u32[]{:S(2)}) collective-permute-start(bf16[640,640]{1,0:T(8,128)(2,1)S(1)} %get-tuple-element.12), channel_id=1, source_target_pairs={{0,1},{1,0},{2,3},{3,2},{4,5},{5,4},{6,7},{7,6},{8,9},{9,8},{10,11... | collective-permute-start | bytes 2457608 | tf_op jit(solution)/shard_map/ppermute | solution.py:185
  52.0 57.5 %copy-start.7 = (f32[20,576]{1,0:T(8,128)S(1)}, f32[20,576]{1,0:T(8,128)}, u32[]{:S(2)}) copy-start(f32[20,576]{1,0:T(8,128)} %master_ref.1) | copy-start | bytes 138244
  52.0 57.5 %copy-start.8 = (f32[20,576]{1,0:T(8,128)S(1)}, f32[20,576]{1,0:T(8,128)}, u32[]{:S(2)}) copy-start(f32[20,576]{1,0:T(8,128)} %one_ref.1) | copy-start | bytes 138244
  52.0 57.5 %copy-start.9 = (f32[20,576]{1,0:T(8,128)S(1)}, f32[20,576]{1,0:T(8,128)}, u32[]{:S(2)}) copy-start(f32[20,576]{1,0:T(8,128)} %two_ref.1) | copy-start | bytes 138244

commit v2 on v1

--- a/solution.py
+++ b/solution.py
@@ -25,27 +25,57 @@
 HALF = H // NC
 XB = HALF // NX
 TILE_ROWS = NZ * 8
+DT = 1152
+STEPS = 3
+CHUNK = DT // STEPS
 f32 = jnp.float32
 bf16 = jnp.bfloat16
-YZ_TYPE = bf16
-
-
-def call(kernel, outs, args, scratch=(), vmem=24, specs=None, flops=0, moved=0):
+Y_TYPE = bf16
+
+
+def call(kernel, outs, args, scratch=(), vmem=24, specs=None, flops=0, moved=0, **kinds):
     return pl.pallas_call(
         kernel,
         out_shape=outs,
         in_specs=specs or [pl.BlockSpec()] * len(args),
+        **kinds,
         scratch_shapes=list(scratch),
         compiler_params=pltpu.CompilerParams(vmem_limit_bytes=vmem * 2**20),
         cost_estimate=pl.CostEstimate(flops=flops, bytes_accessed=moved, transcendentals=0),
     )(*args)
 
 
-def route_kernel(dest_ref, rows_ref, out_ref):
+def teacher_kernel(
+    dest_ref,
+    mean_ref,
+    tokens_hbm,
+    proj_hbm,
+    rotate_hbm,
+    out_ref,
+    tokens_ref,
+    proj_ref,
+    rotate_ref,
+    rows_ref,
+    token_sem,
+    proj_sems,
+    rotate_sems,
+):
+    token_copy = pltpu.make_async_copy(tokens_hbm, tokens_ref, token_sem)
+    token_copy.start()
+    copies = []
+    for k in range(STEPS):
+        part = pl.ds(k * CHUNK, CHUNK)
+        pair = (
+            pltpu.make_async_copy(proj_hbm.at[:, part], proj_ref.at[k], proj_sems.at[k]),
+            pltpu.make_async_copy(rotate_hbm.at[:, part], rotate_ref.at[k], rotate_sems.at[k]),
+        )
+        for copy in pair:
+            copy.start()
+        copies.append(pair)
+
     dest = dest_ref[...]
     spans = lax.broadcasted_iota(jnp.int32, (16, ROWS), 0)
-    named = spans == dest
-    one_hot = jnp.where(named, 1.0, 0.0)
+    one_hot = jnp.where(spans == dest, 1.0, 0.0)
     earlier = (
         lax.broadcasted_iota(jnp.int32, (ROWS, ROWS), 0)
         < lax.broadcasted_iota(jnp.int32, (ROWS, ROWS), 1)
@@ -57,6 +87,21 @@
     )
     rank = jnp.sum(before * one_hot, axis=0, keepdims=True)
     slot = dest * CAP + rank.astype(jnp.int32)
+    rows_ref[:, DW:] = jnp.ones((ROWS, WIDE - DW), bf16)
+
+    token_copy.wait()
+    tokens = tokens_ref[...]
+    total = None
+    for k, (proj_copy, rotate_copy) in enumerate(copies):
+        proj_copy.wait()
+        projected = jnp.dot(tokens, proj_ref[k], preferred_element_type=f32)
+        projected = (projected - mean_ref[:, k * CHUNK : (k + 1) * CHUNK]).astype(bf16)
+        rotate_copy.wait()
+        part = lax.dot_general(
+            projected, rotate_ref[k], (((1,), (1,)), ((), ())), preferred_element_type=f32
+        )
+        total = part if total is None else total + part
+    rows_ref[:, :DW] = total.astype(bf16)
     place = lax.broadcasted_iota(jnp.int32, (SLOTS, ROWS), 0) == slot
     out_ref[...] = jnp.dot(
         jnp.where(place, 1.0, 0.0).astype(bf16), rows_ref[...], preferred_element_type=f32
@@ -76,13 +121,20 @@
         ref[...] = lax.dot_general(pick, act, nt, preferred_element_type=f32).astype(bf16)
 
 
-def error_kernel(arrived_ref, pred_ref, send_ref, error_ref, out_ref):
+def error_kernel(arrived_ref, pred_hbm, send_hbm, error_ref, out_ref, pred_ref, send_ref, sems):
+    pred_copy = pltpu.make_async_copy(pred_hbm, pred_ref, sems.at[0])
+    send_copy = pltpu.make_async_copy(send_hbm, send_ref, sems.at[1])
+    pred_copy.start()
+    send_copy.start()
+    out_ref[:, DW:] = jnp.zeros((HALF, WIDE - DW), bf16)
     live = arrived_ref[:, DW : DW + 1].astype(f32) > 0.5
-    error = jnp.where(live, pred_ref[...] - arrived_ref[:, :DW].astype(f32), 0.0)
+    target = arrived_ref[:, :DW].astype(f32)
+    pred_copy.wait()
+    error = jnp.where(live, pred_ref[...] - target, 0.0)
     error = (error / DW).astype(bf16)
     error_ref[...] = error
+    send_copy.wait()
     out_ref[:, :DW] = jnp.dot(send_ref[...], error, preferred_element_type=f32).astype(bf16)
-    out_ref[:, DW:] = jnp.zeros((HALF, WIDE - DW), bf16)
 
 
 def keep_kernel(keep_ref, error_ref, out_ref):
@@ -110,14 +162,17 @@
         lower = pltpu.roll(sum_ref[at + OWN // 2 : at + OWN, 512:640], 64, axis=1)
         flat_ref[to + 80 : to + 90, :] = jnp.where(left, upper, lower)
         flat_ref[to + 90 : to + 96, :] = jnp.zeros((6, 128), f32)
-        for z in range(NZ):
-            out_ref[z * NY + y] = flat_ref[to + z * 8 : to + z * 8 + 8, :].astype(out_ref.dtype)
-
-
-def adam_kernel(tiles_ref, master_ref, one_ref, two_ref, m_out, f_out, s_out, grad_ref):
+        out_ref[y] = flat_ref[to : to + TILE_ROWS, :].astype(out_ref.dtype)
+
+
+def adam_kernel(tiles_ref, master_ref, one_ref, two_ref, m_out, f_out, s_out, grad_ref, sum_ref):
+    total = tiles_ref[0]
+    for z in range(1, NZ):
+        total = total + tiles_ref[z]
+    sum_ref[...] = total
     for l in range(4):
-        grad_ref[:, l * 128 : (l + 1) * 128] = tiles_ref[l * OWN : (l + 1) * OWN, :]
-    last = tiles_ref[80:90, :]
+        grad_ref[:, l * 128 : (l + 1) * 128] = sum_ref[l * OWN : (l + 1) * OWN, :]
+    last = sum_ref[80:90, :]
     grad_ref[0:10, 512:640] = last
     grad_ref[10:20, 512:640] = pltpu.roll(last, 64, axis=1)
     gradient = grad_ref[:, :DW]
@@ -152,21 +207,35 @@
     moment_two,
 ):
     shape = jax.ShapeDtypeStruct
-    projected = (jnp.dot(tokens, out_proj, preferred_element_type=f32) - phi_mean).astype(bf16)
-    target = jnp.dot(projected, phi_rotate, preferred_element_type=f32).astype(bf16)
-    marked = jnp.pad(target, ((0, 0), (0, WIDE - DW)), constant_values=1.0)
+    whole, far = pl.BlockSpec(), pl.BlockSpec(memory_space=pltpu.HBM)
     outgoing = call(
-        route_kernel,
+        teacher_kernel,
         shape((SLOTS, WIDE), bf16),
-        (destinations.reshape(1, ROWS), marked),
-        flops=2 * SLOTS * ROWS * WIDE,
-        moved=2 * WIDE * (SLOTS + ROWS),
+        (
+            destinations.reshape(1, ROWS),
+            phi_mean.reshape(1, DT),
+            tokens,
+            out_proj,
+            phi_rotate.T,
+        ),
+        specs=[whole, whole, far, far, far],
+        vmem=63,
+        scratch=(
+            pltpu.VMEM((ROWS, DT), bf16),
+            pltpu.VMEM((STEPS, DT, CHUNK), bf16),
+            pltpu.VMEM((STEPS, DW, CHUNK), bf16),
+            pltpu.VMEM((ROWS, WIDE), bf16),
+            pltpu.SemaphoreType.DMA,
+            pltpu.SemaphoreType.DMA((STEPS,)),
+            pltpu.SemaphoreType.DMA((STEPS,)),
+        ),
+        flops=2 * ROWS * DT * (DT + DW) + 2 * SLOTS * ROWS * WIDE,
+        moved=2 * (DT * (DT + DW + ROWS) + SLOTS * WIDE),
     )
     arrived = exchange(outgoing.reshape(NZ, CAP, WIDE), "z").reshape(SLOTS, WIDE)
 
     activated = jax.nn.gelu(student_hidden.astype(f32), approximate=False).astype(bf16)
     core = lax.axis_index("c").astype(jnp.int32).reshape(1)
-    whole = pl.BlockSpec()
     predicted, act_send, act_keep = call(
         student_kernel,
         (shape((SLOTS, DW), f32), shape((HALF, SLOTS), bf16), shape((HALF, SLOTS), bf16)),
@@ -179,6 +248,12 @@
         error_kernel,
         (shape((SLOTS, DW), bf16), shape((HALF, WIDE), bf16)),
         (arrived, predicted, act_send),
+        specs=[whole, far, far],
+        scratch=(
+            pltpu.VMEM((SLOTS, DW), f32),
+            pltpu.VMEM((HALF, SLOTS), bf16),
+            pltpu.SemaphoreType.DMA((2,)),
+        ),
         flops=2 * SLOTS * HALF * DW,
         moved=2 * SLOTS * (WIDE + 3 * DW + HALF) + 2 * HALF * DW,
     )
@@ -196,20 +271,20 @@
     by_x = exchange(chip_sum.reshape(NX, XB, DW), "x")
     tiles = call(
         tile_kernel,
-        shape((NZ * NY, 8, 128), YZ_TYPE),
+        shape((NY, TILE_ROWS, 128), Y_TYPE),
         (by_x,),
         scratch=(pltpu.VMEM((XB, WIDE), f32), pltpu.VMEM((NY * TILE_ROWS, 128), f32)),
         moved=4 * XB * DW * 4,
     )
-    by_yz = exchange(tiles, ("z", "y"))
-    part = by_yz.astype(f32).sum(axis=0)
-    gathered = exchange(jnp.broadcast_to(part, (NZ, 8, 128)), "z").reshape(TILE_ROWS, 128)
+    by_y = exchange(tiles, "y")
+    part = by_y.astype(f32).sum(axis=0)
+    gathered = lax.all_gather(part, "z", axis=0, tiled=False)
     out = shape((OWN, DW), f32)
     return call(
         adam_kernel,
         (out, out, out),
         (gathered, master, moment_one, moment_two),
-        scratch=(pltpu.VMEM((OWN, WIDE), f32),),
+        scratch=(pltpu.VMEM((OWN, WIDE), f32), pltpu.VMEM((TILE_ROWS, 128), f32)),
         moved=4 * OWN * DW * 7,
     )
 

time: 111 us -> 112 us (level)
  the two profiles are of different devices: /device:TPU:8 before, /device:TPU:2 now
where the time goes in v2:
time: 112 us
  blocking collectives  58.5 us (52%)
  waiting for transfers between devices  17.2 us (15%)
  starting transfers between devices  17.1 us (15%)
  Pallas kernels  12.3 us (11%)
  other arithmetic  4.34 us (4%)
  local copies, waits for them, and re-layouts  1.32 us (1%)
    all_to_all x2, blocking collectives, exchange(): return lax.all_to_all(x, axis, split_axis=0, concat_axis=0, tiled=True)  32.9 us
    all_gather x1, blocking collectives, body(): gathered = lax.all_gather(part, 'z', axis=0, tiled=False)  25.6 us
    all_to_all x1, waiting for transfers between devices, exchange(): return lax.all_to_all(x, axis, split_axis=0, concat_axis=0, tiled=True)  15.5 us
    all_to_all x1, starting transfers between devices, exchange(): return lax.all_to_all(x, axis, split_axis=0, concat_axis=0, tiled=True)  15.2 us
    pallas_call x7, Pallas kernels, call(): pl.pallas_call(kernel, out_shape=outs, in_specs=specs or [pl.BlockSpec()]...  12.3 us
    convert_element_type x1, other arithmetic, body(): jax.nn.gelu(student_hidden.astype(f32), approximate=False).astype(bf16)  4.31 us
  transfers between devices with their start and end apart: 2, of which 2 were waited for; matrix products, arithmetic and copies ran while one was open for 4% of the time, Pallas kernels for 3%

profile of v2, /device:TPU:2, one launch (start us, length us, event | category | flops | bytes accessed | tf_op | source)
XLA Modules:
  0.0 111.6 jit_solution(1117884224348843686)
XLA Ops:
  0.6 1.3 %reshape.26.mean_ref = f32[1,1152]{1,0:T(1,128)} reshape(f32[1152]{0:T(1024)} %param.12) | data formatting | bytes 9216 | tf_op jit(solution)/shard_map/reshape | solution.py:216
  1.9 0.0 copy-start.4
  1.9 6.4 %shard_map.122 = bf16[384,640]{1,0:T(8,128)(2,1)} custom-call(s32[1,256]{1,0:T(1,128)} %bitcast.14, f32[1,1152]{1,0:T(1,128)} %reshape.26.mean_ref, bf16[256,1152]{1,0:T(8,128)(2,1)} %tokens_hbm.1, bf16[1152,1152]{1,0:T(8,128)(2,1)} %proj_hbm.1, bf16[576,1152]{1,0:T(8,128)(2,1)} %bitcast.13), custom_call_target="tpu_custom_call" | custom-call | flops 1145044992 | bytes 5062656 | tf_op jit(solution)/shard_map/pallas_call | solution.py:37
  8.3 15.2 %all-to-all-start = ((bf16[12,32,640]{2,1,0:T(8,128)(2,1)}), bf16[12,32,640]{2,1,0:T(8,128)(2,1)S(1)}, u32[]{:S(2)}, u32[]{:S(2)}) async-start(bf16[12,32,640]{2,1,0:T(8,128)(2,1)} %bitcast.12), calls=%async_computation | async-start | bytes 983040 | tf_op jit(solution)/shard_map/all_to_all | solution.py:194
  23.5 0.0 copy-done.4
  23.5 0.0 copy-start.3
  23.5 4.3 %fusion.1.act_ref = bf16[384,1280]{1,0:T(8,128)(2,1)S(1)} fusion(bf16[384,1280]{1,0:T(8,128)(2,1)S(1)} %copy-done.4), kind=kLoop, calls=%fused_computation.4 | loop fusion | flops 32440320 | bytes 1966080 | tf_op jit(solution)/shard_map/convert_element_type | solution.py:237
  27.9 0.0 copy-done.3
  27.9 2.7 %shard_map.121 = (f32[384,576]{1,0:T(8,128)S(1)}, bf16[640,384]{1,0:T(8,128)(2,1)S(1)}, bf16[640,384]{1,0:T(8,128)(2,1)S(1)}) custom-call(s32[1]{0:T(128)} %bitcast.core_ref, bf16[384,1280]{1,0:T(8,128)(2,1)S(1)} %fusion.1.act_ref, bf16[576,1280]{1,0:T(8,128)(2,1)S(1)} %bitcast.11), custom_call_target="tpu_custom_call" | custom-call | flops 1824522240 | bytes 4325376 | tf_op jit(solution)/shard_map/pallas_call | solution.py:37
  30.5 15.5 %all-to-all-done = bf16[12,32,640]{2,1,0:T(8,128)(2,1)S(1)} async-done(((bf16[12,32,640]{2,1,0:T(8,128)(2,1)}), bf16[12,32,640]{2,1,0:T(8,128)(2,1)S(1)}, u32[]{:S(2)}, u32[]{:S(2)}) %all-to-all-start) | async-done | bytes 491552 | tf_op jit(solution)/shard_map/all_to_all | solution.py:194
  46.1 1.5 %shard_map.123 = (bf16[384,576]{1,0:T(8,128)(2,1)S(1)}, bf16[640,640]{1,0:T(8,128)(2,1)S(1)}) custom-call(bf16[384,640]{1,0:T(8,128)(2,1)S(1)} %bitcast.10, f32[384,576]{1,0:T(8,128)S(1)} %get-tuple-element.9.pred_hbm, bf16[640,384]{1,0:T(8,128)(2,1)S(1)} %get-tuple-element.10.send_hbm), custom_call_target="tpu_custom_call" | custom-call | flops 283115520 | bytes 3047424 | tf_op jit(solution)/shard_map/pallas_call | solution.py:37
  47.6 1.9 %collective-permute-start = (bf16[640,640]{1,0:T(8,128)(2,1)S(1)}, bf16[640,640]{1,0:T(8,128)(2,1)S(1)}, u32[]{:S(2)}, u32[]{:S(2)}) collective-permute-start(bf16[640,640]{1,0:T(8,128)(2,1)S(1)} %get-tuple-element.12), channel_id=1, source_target_pairs={{0,1},{1,0},{2,3},{3,2},{4,5},{5,4},{6,7},{7,6},{8,9},{9,8},{10,11... | collective-permute-start | bytes 2457608 | tf_op jit(solution)/shard_map/ppermute | solution.py:260
  49.6 0.6 shard_map.124.own_ref
  50.2 1.7 %collective-permute-done.got_ref = bf16[640,640]{1,0:T(8,128)(2,1)S(1)} collective-permute-done((bf16[640,640]{1,0:T(8,128)(2,1)S(1)}, bf16[640,640]{1,0:T(8,128)(2,1)S(1)}, u32[]{:S(2)}, u32[]{:S(2)}) %collective-permute-start) | collective-permute-done | bytes 819232 | tf_op jit(solution)/shard_map/ppermute | solution.py:260
  51.9 0.1 shard_map.125
  52.0 0.0 copy-start
  52.0 0.0 copy-start.1
  52.0 0.0 copy-start.2
  52.0 16.2 %all_to_all.15.got_ref = bf16[4,160,576]{2,1,0:T(8,128)(2,1)S(1)} all-to-all(bf16[4,160,576]{2,1,0:T(8,128)(2,1)S(1)} %bitcast.8), channel_id=1, replica_groups=mesh['z'=12,'x'=4,'y'=8,'c'=2] {'x'}, dimensions={0} | all-to-all | bytes 1474560 | tf_op jit(solution)/shard_map/all_to_all | solution.py:194
  68.3 0.2 shard_map.126
  68.4 16.7 %all_to_all.16 = bf16[8,96,128]{2,1,0:T(8,128)(2,1)S(1)} all-to-all(bf16[8,96,128]{2,1,0:T(8,128)(2,1)S(1)} %shard_map.126), channel_id=1, replica_groups=mesh['z'=12,'x'=4,'y'=8,'c'=2] {'y'}, dimensions={0} | all-to-all | bytes 393216 | tf_op jit(solution)/shard_map/all_to_all | solution.py:194
  85.1 25.6 %all-gather = f32[1152,128]{1,0:T(8,128)S(1)} all-gather(f32[96,128]{1,0:T(8,128)S(1)} %convert_reduce_fusion), channel_id=2, replica_groups=mesh['z'=12,'x'=4,'y'=8,'c'=2] {'z'}, dimensions={0}, use_global_device_ids=true | all-gather | bytes 638976 | tf_op jit(solution)/shard_map/all_gather | solution.py:281
  110.8 0.0 copy-done
  110.8 0.0 copy-done.1
  110.8 0.0 copy-done.2
  110.8 0.8 shard_map.127
  (1 shorter events, 0.0 us)
Async XLA Ops:
  1.9 21.6 %copy-start.4 = (bf16[384,1280]{1,0:T(8,128)(2,1)S(1)}, bf16[384,1280]{1,0:T(8,128)(2,1)}, u32[]{:S(2)}) copy-start(bf16[384,1280]{1,0:T(8,128)(2,1)} %param.15) | copy-start | bytes 2949124
  8.3 37.7 %all-to-all-start = ((bf16[12,32,640]{2,1,0:T(8,128)(2,1)}), bf16[12,32,640]{2,1,0:T(8,128)(2,1)S(1)}, u32[]{:S(2)}, u32[]{:S(2)}) async-start(bf16[12,32,640]{2,1,0:T(8,128)(2,1)} %bitcast.12), calls=%async_computation | async-start | bytes 983040 | tf_op jit(solution)/shard_map/all_to_all | solution.py:194
  23.5 4.3 %copy-start.3 = (bf16[1280,576]{0,1:T(8,128)(2,1)S(1)}, bf16[1280,576]{0,1:T(8,128)(2,1)}, u32[]{:S(2)}) copy-start(bf16[1280,576]{0,1:T(8,128)(2,1)} %param.16) | copy-start | bytes 4423684
  47.6 4.2 %collective-permute-start = (bf16[640,640]{1,0:T(8,128)(2,1)S(1)}, bf16[640,640]{1,0:T(8,128)(2,1)S(1)}, u32[]{:S(2)}, u32[]{:S(2)}) collective-permute-start(bf16[640,640]{1,0:T(8,128)(2,1)S(1)} %get-tuple-element.12), channel_id=1, source_target_pairs={{0,1},{1,0},{2,3},{3,2},{4,5},{5,4},{6,7},{7,6},{8,9},{9,8},{10,11... | collective-permute-start | bytes 2457608 | tf_op jit(solution)/shard_map/ppermute | solution.py:260
  52.0 58.8 %copy-start = (f32[20,576]{1,0:T(8,128)S(1)}, f32[20,576]{1,0:T(8,128)}, u32[]{:S(2)}) copy-start(f32[20,576]{1,0:T(8,128)} %master_ref.1) | copy-start | bytes 138244
  52.0 58.8 %copy-start.1 = (f32[20,576]{1,0:T(8,128)S(1)}, f32[20,576]{1,0:T(8,128)}, u32[]{:S(2)}) copy-start(f32[20,576]{1,0:T(8,128)} %one_ref.1) | copy-start | bytes 138244
  52.0 58.8 %copy-start.2 = (f32[20,576]{1,0:T(8,128)S(1)}, f32[20,576]{1,0:T(8,128)}, u32[]{:S(2)}) copy-start(f32[20,576]{1,0:T(8,128)} %two_ref.1) | copy-start | bytes 138244

commit v3 on v1

--- a/solution.py
+++ b/solution.py
@@ -30,22 +30,22 @@
 YZ_TYPE = bf16
 
 
-def call(kernel, outs, args, scratch=(), vmem=24, specs=None, flops=0, moved=0):
+def call(kernel, outs, args, scratch=(), vmem=24, specs=None, flops=0, moved=0, **kinds):
     return pl.pallas_call(
         kernel,
         out_shape=outs,
         in_specs=specs or [pl.BlockSpec()] * len(args),
+        **kinds,
         scratch_shapes=list(scratch),
         compiler_params=pltpu.CompilerParams(vmem_limit_bytes=vmem * 2**20),
         cost_estimate=pl.CostEstimate(flops=flops, bytes_accessed=moved, transcendentals=0),
     )(*args)
 
 
-def route_kernel(dest_ref, rows_ref, out_ref):
+def place_kernel(dest_ref, out_ref):
     dest = dest_ref[...]
     spans = lax.broadcasted_iota(jnp.int32, (16, ROWS), 0)
-    named = spans == dest
-    one_hot = jnp.where(named, 1.0, 0.0)
+    one_hot = jnp.where(spans == dest, 1.0, 0.0)
     earlier = (
         lax.broadcasted_iota(jnp.int32, (ROWS, ROWS), 0)
         < lax.broadcasted_iota(jnp.int32, (ROWS, ROWS), 1)
@@ -58,9 +58,14 @@
     rank = jnp.sum(before * one_hot, axis=0, keepdims=True)
     slot = dest * CAP + rank.astype(jnp.int32)
     place = lax.broadcasted_iota(jnp.int32, (SLOTS, ROWS), 0) == slot
-    out_ref[...] = jnp.dot(
-        jnp.where(place, 1.0, 0.0).astype(bf16), rows_ref[...], preferred_element_type=f32
-    ).astype(bf16)
+    out_ref[...] = jnp.where(place, 1.0, 0.0).astype(bf16)
+
+
+def spread_kernel(place_ref, rows_ref, out_ref):
+    place = place_ref[...]
+    out_ref[:, :DW] = jnp.dot(place, rows_ref[...], preferred_element_type=f32).astype(bf16)
+    live = jnp.sum(place.astype(f32), axis=1, keepdims=True)
+    out_ref[:, DW:] = jnp.broadcast_to(live, (SLOTS, WIDE - DW)).astype(bf16)
 
 
 def student_kernel(core_ref, act_ref, adaptor_t_ref, pred_ref, send_ref, keep_ref):
@@ -76,13 +81,25 @@
         ref[...] = lax.dot_general(pick, act, nt, preferred_element_type=f32).astype(bf16)
 
 
-def error_kernel(arrived_ref, pred_ref, send_ref, error_ref, out_ref):
+def error_kernel(
+    arrived_hbm, pred_hbm, send_hbm, error_ref, out_ref, arrived_ref, pred_ref, send_ref, sems
+):
+    arrived_copy = pltpu.make_async_copy(arrived_hbm, arrived_ref, sems.at[2])
+    arrived_copy.start()
+    pred_copy = pltpu.make_async_copy(pred_hbm, pred_ref, sems.at[0])
+    send_copy = pltpu.make_async_copy(send_hbm, send_ref, sems.at[1])
+    pred_copy.start()
+    send_copy.start()
+    out_ref[:, DW:] = jnp.zeros((HALF, WIDE - DW), bf16)
+    arrived_copy.wait()
     live = arrived_ref[:, DW : DW + 1].astype(f32) > 0.5
-    error = jnp.where(live, pred_ref[...] - arrived_ref[:, :DW].astype(f32), 0.0)
+    target = arrived_ref[:, :DW].astype(f32)
+    pred_copy.wait()
+    error = jnp.where(live, pred_ref[...] - target, 0.0)
     error = (error / DW).astype(bf16)
     error_ref[...] = error
+    send_copy.wait()
     out_ref[:, :DW] = jnp.dot(send_ref[...], error, preferred_element_type=f32).astype(bf16)
-    out_ref[:, DW:] = jnp.zeros((HALF, WIDE - DW), bf16)
 
 
 def keep_kernel(keep_ref, error_ref, out_ref):
@@ -152,13 +169,15 @@
     moment_two,
 ):
     shape = jax.ShapeDtypeStruct
+    whole, far = pl.BlockSpec(), pl.BlockSpec(memory_space=pltpu.HBM)
+    place = call(place_kernel, shape((SLOTS, ROWS), bf16), (destinations.reshape(1, ROWS),))
+    place, tokens = lax.optimization_barrier((place, tokens))
     projected = (jnp.dot(tokens, out_proj, preferred_element_type=f32) - phi_mean).astype(bf16)
     target = jnp.dot(projected, phi_rotate, preferred_element_type=f32).astype(bf16)
-    marked = jnp.pad(target, ((0, 0), (0, WIDE - DW)), constant_values=1.0)
     outgoing = call(
-        route_kernel,
+        spread_kernel,
         shape((SLOTS, WIDE), bf16),
-        (destinations.reshape(1, ROWS), marked),
+        (place, target),
         flops=2 * SLOTS * ROWS * WIDE,
         moved=2 * WIDE * (SLOTS + ROWS),
     )
@@ -166,7 +185,6 @@
 
     activated = jax.nn.gelu(student_hidden.astype(f32), approximate=False).astype(bf16)
     core = lax.axis_index("c").astype(jnp.int32).reshape(1)
-    whole = pl.BlockSpec()
     predicted, act_send, act_keep = call(
         student_kernel,
         (shape((SLOTS, DW), f32), shape((HALF, SLOTS), bf16), shape((HALF, SLOTS), bf16)),
@@ -179,6 +197,14 @@
         error_kernel,
         (shape((SLOTS, DW), bf16), shape((HALF, WIDE), bf16)),
         (arrived, predicted, act_send),
+        specs=[far, far, far],
+        vmem=60,
+        scratch=(
+            pltpu.VMEM((SLOTS, WIDE), bf16),
+            pltpu.VMEM((SLOTS, DW), f32),
+            pltpu.VMEM((HALF, SLOTS), bf16),
+            pltpu.SemaphoreType.DMA((3,)),
+        ),
         flops=2 * SLOTS * HALF * DW,
         moved=2 * SLOTS * (WIDE + 3 * DW + HALF) + 2 * HALF * DW,
     )
@@ -203,7 +229,7 @@
     )
     by_yz = exchange(tiles, ("z", "y"))
     part = by_yz.astype(f32).sum(axis=0)
-    gathered = exchange(jnp.broadcast_to(part, (NZ, 8, 128)), "z").reshape(TILE_ROWS, 128)
+    gathered = lax.all_gather(part, "z", axis=0, tiled=True)
     out = shape((OWN, DW), f32)
     return call(
         adam_kernel,

time: 111 us -> 119 us (1.072)
  the two profiles are of different devices: /device:TPU:8 before, /device:TPU:2 now
where the time goes in v3:
time: 119 us; the launch traced here: 118 us
  blocking collectives  64.6 us (54%)
  starting transfers between devices  17.1 us (14%)
  waiting for transfers between devices  13.7 us (12%)
  Pallas kernels  8.85 us (7%)
  other arithmetic  5.48 us (5%)
  local copies, waits for them, and re-layouts  4.48 us (4%)
  matrix products  2.99 us (3%)
    all_to_all x2, blocking collectives, exchange(): return lax.all_to_all(x, axis, split_axis=0, concat_axis=0, tiled=True)  43.5 us
    all_gather x1, blocking collectives, body(): gathered = lax.all_gather(part, 'z', axis=0, tiled=True)  21.1 us
    all_to_all x1, starting transfers between devices, exchange(): return lax.all_to_all(x, axis, split_axis=0, concat_axis=0, tiled=True)  15.2 us
    all_to_all x1, waiting for transfers between devices, exchange(): return lax.all_to_all(x, axis, split_axis=0, concat_axis=0, tiled=True)  12.8 us
    pallas_call x8, Pallas kernels, call(): pl.pallas_call(kernel, out_shape=outs, in_specs=specs or [pl.BlockSpec()]...  8.85 us
    convert_element_type x1, other arithmetic, body(): jax.nn.gelu(student_hidden.astype(f32), approximate=False).astype(bf16)  5.38 us
    unnamed x18, local copies, waits for them, and re-layouts  4.28 us
    dot_general x1, matrix products, body(): jnp.dot(projected, phi_rotate, preferred_element_type=f32).astype(bf16)  2.99 us
  transfers between devices with their start and end apart: 2, of which 2 were waited for; matrix products, arithmetic and copies ran while one was open for 5% of the time, Pallas kernels for 3%

profile of v3, /device:TPU:2, one launch (start us, length us, event | category | flops | bytes accessed | tf_op | source)
XLA Modules:
  0.0 118.0 jit_solution(13239768278821347459)
XLA Ops:
  0.6 0.0 copy-start
  0.6 0.0 copy-start.7
  0.7 0.8 copy-done.7
  1.5 0.2 shard_map.122.place_ref
  1.7 0.7 copy-done
  2.4 3.0 %convolution_convert_fusion = bf16[256,576]{0,1:T(8,128)(2,1)S(1)} fusion(bf16[1152,576]{0,1:T(8,128)(2,1)} %param.13, bf16[256,1152]{1,0:T(8,128)(2,1)} %param.10, bf16[1152,1152]{1,0:T(8,128)(2,1)S(1)} %copy-done, f32[1152]{0:T(1024)} %param.12), kind=kOutput, calls=%fused_computation.36 | convolution fusion | flops 1019953152 | bytes 4870656 | tf_op jit(solution)/shard_map/dot_general | solution.py:176
  5.4 0.2 copy.14.rows_ref
  5.6 1.1 shard_map.123
  6.7 15.2 %all-to-all-start = ((bf16[12,32,640]{2,1,0:T(8,128)(2,1)}), bf16[12,32,640]{2,1,0:T(8,128)(2,1)}, u32[]{:S(2)}, u32[]{:S(2)}) async-start(bf16[12,32,640]{2,1,0:T(8,128)(2,1)} %bitcast.3), calls=%async_computation | async-start | bytes 983040 | tf_op jit(solution)/shard_map/all_to_all | solution.py:156
  21.9 0.0 copy-start.8
  21.9 5.4 %fusion.2.act_ref = bf16[384,1280]{1,0:T(8,128)(2,1)S(1)} fusion(bf16[384,1280]{1,0:T(8,128)(2,1)} %param.15), kind=kLoop, calls=%fused_computation.6 | loop fusion | flops 32440320 | bytes 1966080 | tf_op jit(solution)/shard_map/convert_element_type | solution.py:186
  27.3 0.0 copy-done.8
  27.3 2.6 %shard_map.121 = (f32[384,576]{1,0:T(8,128)S(1)}, bf16[640,384]{1,0:T(8,128)(2,1)S(1)}, bf16[640,384]{1,0:T(8,128)(2,1)S(1)}) custom-call(s32[1]{0:T(128)} %bitcast.core_ref, bf16[384,1280]{1,0:T(8,128)(2,1)S(1)} %fusion.2.act_ref, bf16[576,1280]{1,0:T(8,128)(2,1)S(1)} %bitcast.11), custom_call_target="tpu_custom_call" | custom-call | flops 1824522240 | bytes 4325376 | tf_op jit(solution)/shard_map/pallas_call | solution.py:34
  30.0 0.0 copy-start.1
  30.0 0.9 copy-done.1
  30.9 0.0 copy-start.3
  30.9 0.8 copy-done.3
  31.7 12.8 %all-to-all-done = bf16[12,32,640]{2,1,0:T(8,128)(2,1)} async-done(((bf16[12,32,640]{2,1,0:T(8,128)(2,1)}), bf16[12,32,640]{2,1,0:T(8,128)(2,1)}, u32[]{:S(2)}, u32[]{:S(2)}) %all-to-all-start) | async-done | bytes 491552 | tf_op jit(solution)/shard_map/all_to_all | solution.py:156
  44.5 3.2 %shard_map.124 = (bf16[384,576]{1,0:T(8,128)(2,1)}, bf16[640,640]{1,0:T(8,128)(2,1)}) custom-call(bf16[384,640]{1,0:T(8,128)(2,1)} %bitcast.4.arrived_hbm, f32[384,576]{1,0:T(8,128)} %copy-done.1, bf16[640,384]{1,0:T(8,128)(2,1)} %copy-done.3), custom_call_target="tpu_custom_call" | custom-call | flops 283115520 | bytes 3047424 | tf_op jit(solution)/shard_map/pallas_call | solution.py:34
  47.7 1.9 %collective-permute-start = (bf16[640,640]{1,0:T(8,128)(2,1)}, bf16[640,640]{1,0:T(8,128)(2,1)S(1)}, u32[]{:S(2)}, u32[]{:S(2)}) collective-permute-start(bf16[640,640]{1,0:T(8,128)(2,1)} %get-tuple-element.16), channel_id=1, source_target_pairs={{0,1},{1,0},{2,3},{3,2},{4,5},{5,4},{6,7},{7,6},{8,9},{9,8},{10,11... | collective-permute-start | bytes 2457608 | tf_op jit(solution)/shard_map/ppermute | solution.py:211
  49.6 0.0 copy-start.2
  49.7 1.0 copy-done.2
  50.7 0.6 shard_map.125.own_ref
  51.3 0.9 collective-permute-done.got_ref
  52.2 0.1 shard_map.126
  52.3 0.0 copy-start.4
  52.3 0.0 copy-start.5
  52.3 0.0 copy-start.6
  52.3 16.2 %all_to_all.15.got_ref = bf16[4,160,576]{2,1,0:T(8,128)(2,1)S(1)} all-to-all(bf16[4,160,576]{2,1,0:T(8,128)(2,1)S(1)} %bitcast.9), channel_id=1, replica_groups=mesh['z'=12,'x'=4,'y'=8,'c'=2] {'x'}, dimensions={0} | all-to-all | bytes 1474560 | tf_op jit(solution)/shard_map/all_to_all | solution.py:156
  68.6 0.2 shard_map.127
  68.8 27.3 %all_to_all.16 = bf16[96,8,128]{2,1,0:T(8,128)(2,1)S(1)} all-to-all(bf16[96,8,128]{2,1,0:T(8,128)(2,1)S(1)} %shard_map.127), channel_id=1, replica_groups=mesh['z'=12,'x'=4,'y'=8,'c'=2] {'z','y'}, dimensions={0} | all-to-all | bytes 393216 | tf_op jit(solution)/shard_map/all_to_all | solution.py:156
  96.0 0.1 convert_reduce_fusion
  96.1 21.1 %all_gather.3.tiles_ref = f32[96,128]{1,0:T(8,128)S(1)} all-gather(f32[8,128]{1,0:T(8,128)S(1)} %convert_reduce_fusion), channel_id=1, replica_groups=mesh['z'=12,'x'=4,'y'=8,'c'=2] {'z'}, dimensions={0}, use_global_device_ids=true | all-gather | bytes 53248 | tf_op jit(solution)/shard_map/all_gather | solution.py:232
  117.2 0.0 copy-done.4
  117.2 0.0 copy-done.5
  117.2 0.0 copy-done.6
  117.2 0.7 shard_map.128
Async XLA Ops:
  0.6 1.8 %copy-start = (bf16[1152,1152]{1,0:T(8,128)(2,1)S(1)}, bf16[1152,1152]{1,0:T(8,128)(2,1)}, u32[]{:S(2)}) copy-start(bf16[1152,1152]{1,0:T(8,128)(2,1)} %param.11) | copy-start | bytes 7962628
  0.6 0.8 copy-start.7
  6.7 37.8 %all-to-all-start = ((bf16[12,32,640]{2,1,0:T(8,128)(2,1)}), bf16[12,32,640]{2,1,0:T(8,128)(2,1)}, u32[]{:S(2)}, u32[]{:S(2)}) async-start(bf16[12,32,640]{2,1,0:T(8,128)(2,1)} %bitcast.3), calls=%async_computation | async-start | bytes 983040 | tf_op jit(solution)/shard_map/all_to_all | solution.py:156
  21.9 5.4 %copy-start.8 = (bf16[1280,576]{0,1:T(8,128)(2,1)S(1)}, bf16[1280,576]{0,1:T(8,128)(2,1)}, u32[]{:S(2)}) copy-start(bf16[1280,576]{0,1:T(8,128)(2,1)} %param.16) | copy-start | bytes 4423684
  30.0 0.9 copy-start.1
  30.9 0.8 copy-start.3
  47.7 4.4 %collective-permute-start = (bf16[640,640]{1,0:T(8,128)(2,1)}, bf16[640,640]{1,0:T(8,128)(2,1)S(1)}, u32[]{:S(2)}, u32[]{:S(2)}) collective-permute-start(bf16[640,640]{1,0:T(8,128)(2,1)} %get-tuple-element.16), channel_id=1, source_target_pairs={{0,1},{1,0},{2,3},{3,2},{4,5},{5,4},{6,7},{7,6},{8,9},{9,8},{10,11... | collective-permute-start | bytes 2457608 | tf_op jit(solution)/shard_map/ppermute | solution.py:211
  49.6 1.0 copy-start.2
  52.3 64.9 %copy-start.4 = (f32[20,576]{1,0:T(8,128)S(1)}, f32[20,576]{1,0:T(8,128)}, u32[]{:S(2)}) copy-start(f32[20,576]{1,0:T(8,128)} %master_ref.1) | copy-start | bytes 138244
  52.3 64.9 %copy-start.5 = (f32[20,576]{1,0:T(8,128)S(1)}, f32[20,576]{1,0:T(8,128)}, u32[]{:S(2)}) copy-start(f32[20,576]{1,0:T(8,128)} %one_ref.1) | copy-start | bytes 138244
  52.3 64.9 %copy-start.6 = (f32[20,576]{1,0:T(8,128)S(1)}, f32[20,576]{1,0:T(8,128)}, u32[]{:S(2)}) copy-start(f32[20,576]{1,0:T(8,128)} %two_ref.1) | copy-start | bytes 138244

commit v4 on v3

v4 whole, which is shorter than its diff:
```python
import jax
import jax.numpy as jnp
from jax import lax
from jax.experimental import pallas as pl
from jax.experimental.pallas import tpu as pltpu
from jax.sharding import Mesh, PartitionSpec as P

ADAM_STEP = 1000
beta_first = 0.9
beta_second = 0.999
adam_epsilon = 1e-08
decay_rate = 0.05
learn_rate = 0.001

NZ, NX, NY, NC = 12, 4, 8, 2
CAP = 32
ROWS = 256
SLOTS = NZ * CAP
H = 1280
DW = 576
WIDE = 640
OWN = 20
XB = H // NX
YB = XB // NY
PACKED = 2 * CAP + 8
XROWS = 2 * XB + XB // 4
TILE_ROWS = NZ * 8
EMPTY = 1e30
f32 = jnp.float32
bf16 = jnp.bfloat16
NT = (((1,), (1,)), ((), ()))


def call(kernel, outs, args, scratch=(), vmem=24, specs=None, flops=0, moved=0):
    return pl.pallas_call(
        kernel,
        out_shape=outs,
        in_specs=specs or [pl.BlockSpec()] * len(args),
        scratch_shapes=list(scratch),
        compiler_params=pltpu.CompilerParams(vmem_limit_bytes=vmem * 2**20),
        cost_estimate=pl.CostEstimate(flops=flops, bytes_accessed=moved, transcendentals=0),
    )(*args)


def turn(x, by):
    by = by % 128
    return pltpu.roll(x, by, axis=x.ndim - 1) if by else x


def quarters(parts):
    lane = lax.broadcasted_iota(jnp.int32, parts[0].shape, parts[0].ndim - 1)
    out = parts[3]
    for q in (2, 1, 0):
        out = jnp.where(lane < 32 * (q + 1), parts[q], out)
    return out


def place_kernel(dest_ref, out_ref):
    dest = dest_ref[...]
    spans = lax.broadcasted_iota(jnp.int32, (16, ROWS), 0)
    one_hot = jnp.where(spans == dest, 1.0, 0.0)
    earlier = (
        lax.broadcasted_iota(jnp.int32, (ROWS, ROWS), 0)
        < lax.broadcasted_iota(jnp.int32, (ROWS, ROWS), 1)
    )
    before = jnp.dot(
        one_hot.astype(bf16),
        jnp.where(earlier, 1.0, 0.0).astype(bf16),
        preferred_element_type=f32,
    )
    rank = jnp.sum(before * one_hot, axis=0, keepdims=True)
    slot = dest * CAP + rank.astype(jnp.int32)
    place = lax.broadcasted_iota(jnp.int32, (SLOTS, ROWS), 0) == slot
    out_ref[...] = jnp.where(place, 1.0, 0.0).astype(bf16)


def spread_kernel(place_ref, rows_ref, out_ref, last_ref):
    place = place_ref[...]
    live = jnp.sum(place.astype(f32), axis=1, keepdims=True) > 0.5
    main = jnp.dot(place, rows_ref[:, :512], preferred_element_type=f32)
    main = jnp.where(live, main, EMPTY).astype(bf16)
    last = jnp.dot(place, rows_ref[:, 512:], preferred_element_type=f32)
    last_ref[:, 64:] = jnp.zeros((SLOTS, 64), f32)
    last_ref[:, :64] = jnp.where(live, last, EMPTY)
    last = last_ref[...].reshape(NZ, CAP, 128)
    for c in range(NC):
        packed = quarters(
            [turn(last[:, 8 * q : 8 * q + 8, :], 32 * (q - c)) for q in range(4)]
        ).astype(bf16)
        for z in range(NZ):
            rows = slice(z * CAP, (z + 1) * CAP)
            at = 256 * c
            out_ref[NC * z + c, 0:32, :] = main[rows, at : at + 128]
            out_ref[NC * z + c, 32:64, :] = main[rows, at + 128 : at + 256]
            out_ref[NC * z + c, 64:72, :] = packed[z]


def student_kernel(core_ref, own_ref, other_ref, adaptor_t_ref, pred_ref, last_ref, act_t_ref):
    core = core_ref[0]
    main = adaptor_t_ref[pl.ds(pl.multiple_of(core * 256, 256), 256), :]
    last = adaptor_t_ref[pl.ds(pl.multiple_of(512 + core * 32, 32), 32), :]
    same = lax.broadcasted_iota(jnp.int32, (H, H), 0) == lax.broadcasted_iota(
        jnp.int32, (H, H), 1
    )
    same = jnp.where(same, 1.0, 0.0).astype(bf16)
    for s, ref in enumerate((own_ref, other_ref)):
        rows = slice(s * SLOTS, (s + 1) * SLOTS)
        act = ref[...]
        pred_ref[rows, :] = lax.dot_general(act, main, NT, preferred_element_type=f32)
        last_ref[rows, :] = lax.dot_general(act, last, NT, preferred_element_type=f32)
        act_t_ref[:, rows] = lax.dot_general(same, act, NT, preferred_element_type=f32).astype(
            bf16
        )


def error_kernel(
    core_ref, arrived_ref, pred_ref, last_ref, act_t_ref, out_ref, main_t, last_t, grad_last
):
    core = core_ref[0]
    for s in range(NC):
        source = core if s == 0 else 1 - core
        for z in range(NZ):
            block = arrived_ref[NC * z + source].astype(f32)
            at = s * SLOTS + z * CAP
            main_t[at : at + CAP, 0:128] = block[0:32]
            main_t[at : at + CAP, 128:256] = block[32:64]
            for q in range(4):
                last_t[at + 8 * q : at + 8 * q + 8, :] = turn(block[64:72], -32 * q)

    def scaled(pred, target):
        return (jnp.where(target < 0.1 * EMPTY, pred - target, 0.0) / DW).astype(bf16)

    act_t = act_t_ref[...]
    grad = jnp.dot(
        act_t, scaled(pred_ref[...], main_t[...]), preferred_element_type=f32
    ).astype(bf16)
    grad_last[:, :32] = jnp.dot(
        act_t, scaled(last_ref[...], last_t[:, :32]), preferred_element_type=f32
    )
    for x in range(NX):
        at = x * XB
        out_ref[x, 0:XB, :] = grad[at : at + XB, 0:128]
        out_ref[x, XB : 2 * XB, :] = grad[at : at + XB, 128:256]
        out_ref[x, 2 * XB :, :] = quarters(
            [turn(grad_last[at + 80 * q : at + 80 * q + 80, :], 32 * q) for q in range(4)]
        ).astype(bf16)


def tile_kernel(got_ref, out_ref, sum_ref, flat_ref):
    total = got_ref[0].astype(f32)
    for x in range(1, NX):
        total = total + got_ref[x].astype(f32)
    sum_ref[...] = total
    for y in range(NY):
        to, at = y * TILE_ROWS, y * YB
        flat_ref[to : to + 40, :] = sum_ref[at : at + 40, :]
        flat_ref[to + 40 : to + 80, :] = sum_ref[XB + at : XB + at + 40, :]
        rest = 2 * XB + (y % 2) * 40
        flat_ref[to + 80 : to + 90, :] = quarters(
            [
                turn(sum_ref[rest + 10 * q : rest + 10 * q + 10, :], 32 * (q - y // 2))
                for q in range(4)
            ]
        )
        flat_ref[to + 90 : to + 96, :] = jnp.zeros((6, 128), f32)
        for z in range(NZ):
            out_ref[z * NY + y] = flat_ref[to + z * 8 : to + z * 8 + 8, :].astype(out_ref.dtype)


def adam_kernel(
    core_ref, tiles_ref, master_ref, one_ref, two_ref, m_out, f_out, s_out, grad_ref, flat_ref
):
    first_core = core_ref[0] == 0
    upper, lower = [], []
    for c in range(NC):
        base = c * TILE_ROWS
        for z in range(NZ):
            flat_ref[base + z * 8 : base + z * 8 + 8, :] = tiles_ref[NC * z + c]
        for part in range(2):
            at = base + 40 * part
            to = 256 * c + 128 * part
            grad_ref[:, to : to + 128] = jnp.where(
                first_core, flat_ref[at : at + 20, :], flat_ref[at + 20 : at + 40, :]
            )
        packed = flat_ref[base + 80 : base + 90, :]
        upper.append(jnp.where(first_core, turn(packed, 32 * c), turn(packed, 32 * c - 64)))
        lower.append(jnp.where(first_core, turn(packed, 32 * c - 32), turn(packed, 32 * c - 96)))
    left = lax.broadcasted_iota(jnp.int32, (10, 128), 1) < 32
    grad_ref[0:10, 512:640] = jnp.where(left, upper[0], upper[1])
    grad_ref[10:20, 512:640] = jnp.where(left, lower[0], lower[1])
    gradient = grad_ref[:, :DW]
    master = master_ref[...]
    first_new = beta_first * one_ref[...] + (1.0 - beta_first) * gradient
    second_new = beta_second * two_ref[...] + (1.0 - beta_second) * gradient * gradient
    bias_first = 1.0 - beta_first**ADAM_STEP
    bias_second = 1.0 - beta_second**ADAM_STEP
    update_dir = (
        first_new / bias_first / (jnp.sqrt(second_new / bias_second) + adam_epsilon)
        + decay_rate * master
    )
    m_out[...] = master - learn_rate * update_dir
    f_out[...] = first_new
    s_out[...] = second_new


def exchange(x, axis):
    return lax.all_to_all(x, axis, split_axis=0, concat_axis=0, tiled=True)


def body(
    tokens,
    out_proj,
    phi_mean,
    phi_rotate,
    destinations,
    student_hidden,
    adaptor,
    master,
    moment_one,
    moment_two,
):
    shape = jax.ShapeDtypeStruct
    whole, scalar = pl.BlockSpec(), pl.BlockSpec(memory_space=pltpu.SMEM)
    core = lax.axis_index("c").astype(jnp.int32).reshape(1)
    place = call(place_kernel, shape((SLOTS, ROWS), bf16), (destinations.reshape(1, ROWS),))
    place, tokens = lax.optimization_barrier((place, tokens))
    projected = (jnp.dot(tokens, out_proj, preferred_element_type=f32) - phi_mean).astype(bf16)
    target = jnp.dot(projected, phi_rotate, preferred_element_type=f32).astype(bf16)
    outgoing = call(
        spread_kernel,
        shape((NZ * NC, PACKED, 128), bf16),
        (place, target),
        scratch=(pltpu.VMEM((SLOTS, 128), f32),),
        flops=2 * SLOTS * ROWS * WIDE,
        moved=2 * WIDE * (SLOTS + ROWS),
    )
    arrived = exchange(outgoing, ("z", "c"))
    activated = jax.nn.gelu(student_hidden.astype(f32), approximate=False).astype(bf16)
    other = lax.ppermute(activated, "c", [(0, 1), (1, 0)])
    both = NC * SLOTS
    predicted, predicted_last, act_t = call(
        student_kernel,
        (shape((both, 256), f32), shape((both, 32), f32), shape((H, both), bf16)),
        (core, activated, other, adaptor.T),
        specs=[scalar, whole, whole, whole],
        flops=2 * both * H * (288 + H),
        moved=2 * both * H * 2 + 2 * H * DW + 4 * both * 384,
    )
    partial = call(
        error_kernel,
        shape((NX, XROWS, 128), bf16),
        (core, arrived, predicted, predicted_last, act_t),
        specs=[scalar, whole, whole, whole, whole],
        scratch=(
            pltpu.VMEM((both, 256), f32),
            pltpu.VMEM((both, 128), f32),
            pltpu.VMEM((H, 128), f32),
        ),
        flops=2 * both * H * 384,
        moved=2 * both * H + 4 * both * 384,
    )
    by_x = exchange(partial, "x")
    tiles = call(
        tile_kernel,
        shape((NZ * NY, 8, 128), bf16),
        (by_x,),
        scratch=(pltpu.VMEM((XROWS, 128), f32), pltpu.VMEM((NY * TILE_ROWS, 128), f32)),
        moved=4 * XROWS * 128 * 4,
    )
    by_yz = exchange(tiles, ("z", "y"))
    part = by_yz.astype(f32).sum(axis=0)
    gathered = exchange(jnp.broadcast_to(part, (NZ * NC, 8, 128)), ("z", "c"))
    out = shape((OWN, DW), f32)
    return call(
        adam_kernel,
        (out, out, out),
        (core, gathered, master, moment_one, moment_two),
        specs=[scalar, whole, whole, whole, whole],
        scratch=(pltpu.VMEM((OWN, WIDE), f32), pltpu.VMEM((NC * TILE_ROWS, 128), f32)),
        moved=4 * OWN * DW * 7,
    )


def solution(mesh):
    grid = Mesh(mesh.devices.reshape(NZ, NX, NY, NC), ("z", "x", "y", "c"))
    rows = P(("z", "x", "y", "c"), None)
    state = P(("x", "y", "c"), None)
    in_specs = (rows, P(), P(), P(), rows, rows, P(), state, state, state)
    return jax.shard_map(
        body, mesh=grid, in_specs=in_specs, out_specs=(state, state, state), check_vma=False
    )
```

time: 119 us -> 115 us (0.966)
  the two profiles are of different devices: /device:TPU:2 before, /device:TPU:1 now
where the time goes in v4:
time: 115 us
  blocking collectives  59.5 us (52%)
  starting transfers between devices  18.7 us (16%)
  waiting for transfers between devices  10 us (9%)
  Pallas kernels  9.92 us (9%)
  local copies, waits for them, and re-layouts  6.47 us (6%)
  other arithmetic  6.24 us (5%)
  matrix products  2.98 us (3%)
    all_to_all x3, blocking collectives, exchange(): return lax.all_to_all(x, axis, split_axis=0, concat_axis=0, tiled=True)  59.5 us
    ppermute x1, starting transfers between devices, body(): other = lax.ppermute(activated, 'c', [(0, 1), (1, 0)])  12.4 us
    all_to_all x1, waiting for transfers between devices, exchange(): return lax.all_to_all(x, axis, split_axis=0, concat_axis=0, tiled=True)  10 us
    pallas_call x6, Pallas kernels, call(): pl.pallas_call(kernel, out_shape=outs, in_specs=specs or [pl.BlockSpec()]...  9.92 us
    all_to_all x1, starting transfers between devices, exchange(): return lax.all_to_all(x, axis, split_axis=0, concat_axis=0, tiled=True)  6.32 us
    unnamed x22, local copies, waits for them, and re-layouts  6.26 us
    convert_element_type x1, other arithmetic, body(): jax.nn.gelu(student_hidden.astype(f32), approximate=False).astype(bf16)  6.13 us
    dot_general x1, matrix products, body(): jnp.dot(projected, phi_rotate, preferred_element_type=f32).astype(bf16)  2.98 us
  transfers between devices with their start and end apart: 2, of which 1 were waited for; matrix products, arithmetic and copies ran while one was open for 3% of the time, Pallas kernels for 7%

profile of v4, /device:TPU:1, one launch (start us, length us, event | category | flops | bytes accessed | tf_op | source)
XLA Modules:
  0.0 114.6 jit_solution(6914973586639279047)
XLA Ops:
  0.6 0.0 copy-start
  0.6 0.0 copy-start.8
  0.7 0.0 copy-start.10
  0.7 6.1 %fusion.2.own_ref = bf16[384,1280]{1,0:T(8,128)(2,1)} fusion(bf16[384,1280]{1,0:T(8,128)(2,1)} %param.15), kind=kLoop, calls=%fused_computation.6 | loop fusion | flops 32440320 | bytes 1966080 | tf_op jit(solution)/shard_map/convert_element_type | solution.py:238
  6.8 12.4 %collective-permute-start = (bf16[384,1280]{1,0:T(8,128)(2,1)}, bf16[384,1280]{1,0:T(8,128)(2,1)}, u32[]{:S(2)}, u32[]{:S(2)}) collective-permute-start(bf16[384,1280]{1,0:T(8,128)(2,1)} %fusion.2.own_ref), channel_id=1, source_target_pairs={{0,1},{1,0},{2,3},{3,2},{4,5},{5,4},{6,7},{7,6},{8,9},{9,8},{10,11... | collective-permute-start | bytes 2949128 | tf_op jit(solution)/shard_map/ppermute | solution.py:239
  19.2 0.0 copy-done.8
  19.2 0.2 shard_map.121.place_ref
  19.4 0.0 copy-done
  19.4 0.0 copy-done.10
  19.5 3.0 %convolution_convert_fusion = bf16[256,576]{0,1:T(8,128)(2,1)S(1)} fusion(bf16[1152,576]{0,1:T(8,128)(2,1)} %param.13, bf16[256,1152]{1,0:T(8,128)(2,1)} %param.10, bf16[1152,1152]{1,0:T(8,128)(2,1)S(1)} %copy-done, f32[1152]{0:T(1024)S(1)} %copy-done.10), kind=kOutput, calls=%fused_computation.36 | convolution fusion | flops 1019953152 | bytes 4870656 | tf_op jit(solution)/shard_map/dot_general | solution.py:228
  22.4 0.2 copy.14.rows_ref
  22.6 1.2 %shard_map.122 = bf16[24,72,128]{2,1,0:T(8,128)(2,1)} custom-call(bf16[384,256]{1,0:T(8,128)(2,1)S(1)} %shard_map.121.place_ref, bf16[256,576]{1,0:T(8,128)(2,1)S(1)} %copy.14.rows_ref), custom_call_target="tpu_custom_call" | custom-call | flops 125829120 | bytes 819200 | tf_op jit(solution)/shard_map/pallas_call | solution.py:35
  23.9 6.3 %all-to-all-start = ((bf16[24,72,128]{2,1,0:T(8,128)(2,1)}), bf16[24,72,128]{2,1,0:T(8,128)(2,1)S(1)}, u32[]{:S(2)}, u32[]{:S(2)}) async-start(bf16[24,72,128]{2,1,0:T(8,128)(2,1)} %shard_map.122), calls=%async_computation | async-start | bytes 884736 | tf_op jit(solution)/shard_map/all_to_all | solution.py:207
  30.2 0.0 collective-permute-done.other_ref
  30.2 0.0 copy-start.9
  30.2 1.4 %copy-done.9 = bf16[1280,576]{0,1:T(8,128)(2,1)S(1)} copy-done((bf16[1280,576]{0,1:T(8,128)(2,1)S(1)}, bf16[1280,576]{0,1:T(8,128)(2,1)}, u32[]{:S(2)}) %copy-start.9) | copy-done | bytes 1474584
  31.6 6.1 %shard_map.123 = (f32[768,256]{1,0:T(8,128)S(1)}, f32[768,32]{1,0:T(8,128)S(1)}, bf16[1280,768]{1,0:T(8,128)(2,1)S(1)}) custom-call(s32[1]{0:T(128)} %bitcast.core_ref, bf16[384,1280]{1,0:T(8,128)(2,1)} %fusion.2.own_ref, bf16[384,1280]{1,0:T(8,128)(2,1)} %collective-permute-done.other_ref, bf16[576,1280]{1,0:T(8,128)(2,1)S(1)} %bitcast.7), custom_call_target="tpu_custom_call" | custom-call | flops 3082813440 | bytes 6586368 | tf_op jit(solution)/shard_map/pallas_call | solution.py:35
  37.7 0.0 copy-start.1
  37.7 1.3 %copy-done.1 = bf16[1280,768]{1,0:T(8,128)(2,1)} copy-done((bf16[1280,768]{1,0:T(8,128)(2,1)}, bf16[1280,768]{1,0:T(8,128)(2,1)S(1)}, u32[]{:S(2)}) %copy-start.1) | copy-done | bytes 1966104
  38.9 0.0 copy-start.3
  38.9 0.9 copy-done.3
  39.8 10.0 %all-to-all-done.arrived_ref = bf16[24,72,128]{2,1,0:T(8,128)(2,1)S(1)} async-done(((bf16[24,72,128]{2,1,0:T(8,128)(2,1)}), bf16[24,72,128]{2,1,0:T(8,128)(2,1)S(1)}, u32[]{:S(2)}, u32[]{:S(2)}) %all-to-all-start) | async-done | bytes 442400 | tf_op jit(solution)/shard_map/all_to_all | solution.py:207
  49.9 0.0 copy-start.2
  49.9 1.5 %copy-done.2 = bf16[1280,768]{1,0:T(8,128)(2,1)S(1)} copy-done((bf16[1280,768]{1,0:T(8,128)(2,1)S(1)}, bf16[1280,768]{1,0:T(8,128)(2,1)}, u32[]{:S(2)}) %copy-start.2) | copy-done | bytes 1966104
  51.4 0.0 copy-start.4
  51.4 1.1 copy-done.4
  52.6 1.4 %shard_map.124 = bf16[4,720,128]{2,1,0:T(8,128)(2,1)S(1)} custom-call(s32[1]{0:T(128)} %bitcast.core_ref, bf16[24,72,128]{2,1,0:T(8,128)(2,1)S(1)} %all-to-all-done.arrived_ref, f32[768,256]{1,0:T(8,128)S(1)} %copy-done.4, f32[768,32]{1,0:T(8,128)S(1)} %get-tuple-element.11.last_ref, bf16[1280,768]{1,0:T(8,128)(2,1)S(1)} %copy-done.2), custom_call_target="tpu_custom_call" | custom-call | flops 754974720 | bytes 3145728 | tf_op jit(solution)/shard_map/pallas_call | solution.py:35
  54.0 0.0 copy-start.5
  54.0 0.0 copy-start.6
  54.0 0.0 copy-start.7
  54.0 12.7 %all_to_all.20.got_ref = bf16[4,720,128]{2,1,0:T(8,128)(2,1)S(1)} all-to-all(bf16[4,720,128]{2,1,0:T(8,128)(2,1)S(1)} %shard_map.124), channel_id=1, replica_groups=mesh['z'=12,'x'=4,'y'=8,'c'=2] {'x'}, dimensions={0} | all-to-all | bytes 1474560 | tf_op jit(solution)/shard_map/all_to_all | solution.py:207
  66.8 0.2 shard_map.125
  67.0 30.2 %all_to_all.21 = bf16[96,8,128]{2,1,0:T(8,128)(2,1)S(1)} all-to-all(bf16[96,8,128]{2,1,0:T(8,128)(2,1)S(1)} %shard_map.125), channel_id=1, replica_groups=mesh['z'=12,'x'=4,'y'=8,'c'=2] {'z','y'}, dimensions={0} | all-to-all | bytes 393216 | tf_op jit(solution)/shard_map/all_to_all | solution.py:207
  97.1 0.1 convert_reduce_fusion
  97.2 16.6 %all_to_all.22.tiles_ref = f32[24,8,128]{2,1,0:T(8,128)S(1)} all-to-all(f32[24,8,128]{2,1,0:T(8,128)S(1)} %broadcast_in_dim.4), channel_id=1, replica_groups=mesh['z'=12,'x'=4,'y'=8,'c'=2] {'z','c'}, dimensions={0} | all-to-all | bytes 196608 | tf_op jit(solution)/shard_map/all_to_all | solution.py:207
  113.9 0.0 copy-done.5
  113.9 0.0 copy-done.6
  113.9 0.0 copy-done.7
  113.9 0.8 shard_map.126
  (1 shorter events, 0.0 us)
Async XLA Ops:
  0.6 18.8 %copy-start = (bf16[1152,1152]{1,0:T(8,128)(2,1)S(1)}, bf16[1152,1152]{1,0:T(8,128)(2,1)}, u32[]{:S(2)}) copy-start(bf16[1152,1152]{1,0:T(8,128)(2,1)} %param.11) | copy-start | bytes 7962628
  0.6 18.5 %copy-start.8 = (s32[256,1]{0,1:T(1,128)S(1)}, s32[256,1]{0,1:T(1,128)}, u32[]{:S(2)}) copy-start(s32[256,1]{0,1:T(1,128)} %param.14) | copy-start | bytes 3076
  0.7 18.8 %copy-start.10 = (f32[1152]{0:T(1024)S(1)}, f32[1152]{0:T(1024)}, u32[]{:S(2)}) copy-start(f32[1152]{0:T(1024)} %param.12) | copy-start | bytes 13828
  6.8 23.4 %collective-permute-start = (bf16[384,1280]{1,0:T(8,128)(2,1)}, bf16[384,1280]{1,0:T(8,128)(2,1)}, u32[]{:S(2)}, u32[]{:S(2)}) collective-permute-start(bf16[384,1280]{1,0:T(8,128)(2,1)} %fusion.2.own_ref), channel_id=1, source_target_pairs={{0,1},{1,0},{2,3},{3,2},{4,5},{5,4},{6,7},{7,6},{8,9},{9,8},{10,11... | collective-permute-start | bytes 2949128 | tf_op jit(solution)/shard_map/ppermute | solution.py:239
  23.9 26.0 %all-to-all-start = ((bf16[24,72,128]{2,1,0:T(8,128)(2,1)}), bf16[24,72,128]{2,1,0:T(8,128)(2,1)S(1)}, u32[]{:S(2)}, u32[]{:S(2)}) async-start(bf16[24,72,128]{2,1,0:T(8,128)(2,1)} %shard_map.122), calls=%async_computation | async-start | bytes 884736 | tf_op jit(solution)/shard_map/all_to_all | solution.py:207
  30.2 1.4 %copy-start.9 = (bf16[1280,576]{0,1:T(8,128)(2,1)S(1)}, bf16[1280,576]{0,1:T(8,128)(2,1)}, u32[]{:S(2)}) copy-start(bf16[1280,576]{0,1:T(8,128)(2,1)} %param.16) | copy-start | bytes 4423684
  37.7 1.3 %copy-start.1 = (bf16[1280,768]{1,0:T(8,128)(2,1)}, bf16[1280,768]{1,0:T(8,128)(2,1)S(1)}, u32[]{:S(2)}) copy-start(bf16[1280,768]{1,0:T(8,128)(2,1)S(1)} %get-tuple-element.12.act_t_ref) | copy-start | bytes 5898244
  38.9 0.9 copy-start.3
  49.9 1.5 %copy-start.2 = (bf16[1280,768]{1,0:T(8,128)(2,1)S(1)}, bf16[1280,768]{1,0:T(8,128)(2,1)}, u32[]{:S(2)}) copy-start(bf16[1280,768]{1,0:T(8,128)(2,1)} %copy-done.1) | copy-start | bytes 5898244
  51.4 1.1 copy-start.4
  54.0 59.9 %copy-start.5 = (f32[20,576]{1,0:T(8,128)S(1)}, f32[20,576]{1,0:T(8,128)}, u32[]{:S(2)}) copy-start(f32[20,576]{1,0:T(8,128)} %master_ref.1) | copy-start | bytes 138244
  54.0 59.9 %copy-start.6 = (f32[20,576]{1,0:T(8,128)S(1)}, f32[20,576]{1,0:T(8,128)}, u32[]{:S(2)}) copy-start(f32[20,576]{1,0:T(8,128)} %one_ref.1) | copy-start | bytes 138244
  54.0 59.9 %copy-start.7 = (f32[20,576]{1,0:T(8,128)S(1)}, f32[20,576]{1,0:T(8,128)}, u32[]{:S(2)}) copy-start(f32[20,576]{1,0:T(8,128)} %two_ref.1) | copy-start | bytes 138244
